TPU v7x, 512 devices: a whole 4x4x16 slice. The times are simulated.
512 devices in a mesh: freq: 8 (over y, x_lo), cells: 64 (over z, x_hi, core).
Axes of the slice: x: 4 (x_hi: 2, x_lo: 2; x = x_hi * 2 + x_lo), y: 4, z: 16, core: 2. Of those that a mesh axis runs over, the one named last changes fastest.
Arguments:
- jacobian_tiles: bfloat16 [8, 192, 20, 128, 128], P('freq', 'cells'), may hold values from -0.29882812 to 0.29882812
- tip_lists: int32 [192, 20], P('cells'), may hold values from 0 to 31, as said below
- counts: int32 [192], P('cells'), may hold values from 1 to 20, as said below
- residual: bfloat16 [8, 4096], P('freq'), may hold values from -6 to 6
Outputs:
- normal_band: float32 [192, 5, 3, 128, 128], P('cells', None, None, 'freq')
- gradient: float32 [24576], P('cells')
Inputs may be any that keep to these rules, and one draw needn't show every extreme that they name: `tip_lists`: each cell block's list names 20 different tip blocks, consecutive modulo 32. The first counts[a] slots of cell block a are live.
All inputs are finite; a program needn't handle non-finite values.
Results may differ from a plain program's by a relative error of at most 0.0003.
Values may be sent and summed in bfloat16 or wider, within the bound.
A program may use at most 64 MiB of HBM per device.

v0:
```python
import jax
import jax.numpy as jnp
from jax import lax
from jax.sharding import PartitionSpec as P

SHIFTS = 4


def shifted(x, axis, by):
    size = lax.axis_size(axis)
    return lax.ppermute(x, axis, [(i, (i + by) % size) for i in range(size)])


def live_of(counts, slot_count):
    slot_ids = jnp.arange(slot_count, dtype=jnp.int32)
    return slot_ids[None, :] < counts[:, None]


def panel_products(local_tiles, local_tips, local_live, far_tiles, far_tips, far_counts):
    far_live = live_of(far_counts, far_tips.shape[1])
    matches = local_tips[:, :, None, None] == far_tips[None, None, :, :]
    matches = matches & local_live[:, :, None, None] & far_live[None, None, :, :]
    matches = matches.astype(jnp.bfloat16)
    matched = jnp.einsum(
        "apbq,fbqik->fabpik", matches, far_tiles, preferred_element_type=jnp.float32
    ).astype(jnp.bfloat16)
    return jnp.einsum(
        "fapij,fabpik->abjk", local_tiles, matched, preferred_element_type=jnp.float32
    )


def on_device(jacobian_tiles, tip_lists, counts, residual):
    tile_width = jacobian_tiles.shape[-1]
    slot_count = jacobian_tiles.shape[2]
    block_count = jacobian_tiles.shape[1]
    local_live = live_of(counts, slot_count)
    own_panel = (jacobian_tiles, tip_lists, counts)
    panel_now = own_panel
    blocks = []
    for offset in range(SHIFTS + 1):
        if offset > 0:
            panel_now = shifted((panel_now[0], panel_now[1], panel_now[2]), "cells", -1)
        products = panel_products(
            jacobian_tiles, tip_lists, local_live, panel_now[0], panel_now[1], panel_now[2]
        )
        blocks.append(products)
    stacked = jnp.stack(blocks, axis=1)
    normal_band = lax.psum_scatter(stacked, "freq", scatter_dimension=3, tiled=True)
    tip_count = residual.shape[1] // tile_width
    tip_ids = jnp.arange(tip_count, dtype=jnp.int32)
    onehot = ((tip_lists[:, :, None] == tip_ids[None, None, :]) & local_live[:, :, None]).astype(
        jnp.bfloat16
    )
    resid_blocks = residual.reshape(residual.shape[0], tip_count, tile_width)
    picked = jnp.einsum(
        "apt,fti->fapi", onehot, resid_blocks, preferred_element_type=jnp.float32
    ).astype(jnp.bfloat16)
    grad_part = jnp.einsum(
        "fapij,fapi->aj", jacobian_tiles, picked, preferred_element_type=jnp.float32
    )
    gradient = lax.psum(grad_part, "freq")
    return (normal_band, gradient.reshape(block_count * tile_width))


def solution(mesh):
    placed = (P("freq", "cells", None, None, None), P("cells", None), P("cells"), P("freq", None))
    return jax.shard_map(
        on_device,
        mesh=mesh,
        in_specs=placed,
        out_specs=(P("cells", None, None, "freq", None), P("cells")),
        check_vma=False,
    )
```

profile of v0, /device:TPU:1, one launch (start us, length us, event | category | flops | bytes accessed | tf_op | source)
XLA Modules:
  0.0 363.6 jit_solution(12629005852515925661)
XLA Ops:
  7.2 8.8 %collective-permute-start.2 = (bf16[1,3,20,128,128]{4,3,2,1,0:T(8,128)(2,1)}, bf16[1,3,20,128,128]{4,3,2,1,0:T(8,128)(2,1)S(1)}, u32[]{:S(2)}, u32[]{:S(2)}) collective-permute-start(bf16[1,3,20,128,128]{4,3,2,1,0:T(8,128)(2,1)} %param.4), channel_id=1, source_target_pairs={{0,63},{1,0},{2,1},{3,2},{4,3},{5,4},{6,5},{7,6},{8,7},{9,8},{10,9... | collective-permute-start | bytes 5898248 | tf_op jit(solution)/shard_map/ppermute | solution.py:11
  16.0 19.8 %collective-permute-done.2 = bf16[1,3,20,128,128]{4,3,2,1,0:T(8,128)(2,1)S(1)} collective-permute-done((bf16[1,3,20,128,128]{4,3,2,1,0:T(8,128)(2,1)}, bf16[1,3,20,128,128]{4,3,2,1,0:T(8,128)(2,1)S(1)}, u32[]{:S(2)}, u32[]{:S(2)}) %collective-permute-start.2) | collective-permute-done | bytes 1966112 | tf_op jit(solution)/shard_map/ppermute | solution.py:11
  35.8 10.6 %collective-permute-start.5 = (bf16[1,3,20,128,128]{4,3,2,1,0:T(8,128)(2,1)S(1)}, bf16[1,3,20,128,128]{4,3,2,1,0:T(8,128)(2,1)S(1)}, u32[]{:S(2)}, u32[]{:S(2)}) collective-permute-start(bf16[1,3,20,128,128]{4,3,2,1,0:T(8,128)(2,1)S(1)} %collective-permute-done.2), channel_id=1, source_target_pairs={{0,63},{1,0},{2,1},{3,2},{4,3},{5,4},{6,5},{7,6},{8,7},{9,8},{10,9... | collective-permute-start | bytes 5898248 | tf_op jit(solution)/shard_map/ppermute | solution.py:11
  46.4 7.3 %collective-permute-start = (s32[3,20]{1,0:T(4,128)}, s32[3,20]{1,0:T(4,128)S(1)}, u32[]{:S(2)}, u32[]{:S(2)}) collective-permute-start(s32[3,20]{1,0:T(4,128)} %param.5), channel_id=1, source_target_pairs={{0,63},{1,0},{2,1},{3,2},{4,3},{5,4},{6,5},{7,6},{8,7},{9,8},{10,9... | collective-permute-start | bytes 728 | tf_op jit(solution)/shard_map/ppermute | solution.py:11
  56.4 4.0 %convert_bitcast_fusion.4 = bf16[3,3,20,128,128]{4,2,3,0,1:T(8,128)(2,1)S(1)} fusion(bf16[3,20,128,128,1]{3,2,1,0,4:T(8,128)(2,1)} %bitcast.183, s32[3,20]{1,0:T(4,128)} %param.5, pred[3,20]{1,0:T(4,128)(4,1)S(1)} %iota_compare_fusion.5), kind=kOutput, calls=%fused_computation.4 | convolution fusion | flops 120924720 | bytes 7864620 | tf_op jit(solution)/shard_map/apbq,fbqik->fabpik/dot_general | solution.py:24
  60.4 2.8 collective-permute-done.5
  63.2 12.6 %collective-permute-start.8 = (bf16[1,3,20,128,128]{4,3,2,1,0:T(8,128)(2,1)S(1)}, bf16[1,3,20,128,128]{4,3,2,1,0:T(8,128)(2,1)S(1)}, u32[]{:S(2)}, u32[]{:S(2)}) collective-permute-start(bf16[1,3,20,128,128]{4,3,2,1,0:T(8,128)(2,1)S(1)} %collective-permute-done.5), channel_id=1, source_target_pairs={{0,63},{1,0},{2,1},{3,2},{4,3},{5,4},{6,5},{7,6},{8,7},{9,8},{10,9... | collective-permute-start | bytes 5898248 | tf_op jit(solution)/shard_map/ppermute | solution.py:11
  75.8 3.0 fusion.31
  78.9 7.4 %collective-permute-start.4 = (s32[3]{0:T(128)S(1)}, s32[3]{0:T(128)S(1)}, u32[]{:S(2)}, u32[]{:S(2)}) collective-permute-start(s32[3]{0:T(128)S(1)} %collective-permute-done.1), channel_id=1, source_target_pairs={{0,63},{1,0},{2,1},{3,2},{4,3},{5,4},{6,5},{7,6},{8,7},{9,8},{10,9... | collective-permute-start | bytes 44 | tf_op jit(solution)/shard_map/ppermute | solution.py:11
  86.4 4.4 %collective-permute-done.4 = s32[3]{0:T(128)S(1)} collective-permute-done((s32[3]{0:T(128)S(1)}, s32[3]{0:T(128)S(1)}, u32[]{:S(2)}, u32[]{:S(2)}) %collective-permute-start.4) | collective-permute-done | bytes 44 | tf_op jit(solution)/shard_map/ppermute | solution.py:11
  90.8 14.7 %collective-permute-start.7 = (s32[3]{0:T(128)S(1)}, s32[3]{0:T(128)S(1)}, u32[]{:S(2)}, u32[]{:S(2)}) collective-permute-start(s32[3]{0:T(128)S(1)} %collective-permute-done.4), channel_id=1, source_target_pairs={{0,63},{1,0},{2,1},{3,2},{4,3},{5,4},{6,5},{7,6},{8,7},{9,8},{10,9... | collective-permute-start | bytes 44 | tf_op jit(solution)/shard_map/ppermute | solution.py:11
  105.5 7.5 %collective-permute-start.3 = (s32[3,20]{1,0:T(4,128)S(1)}, s32[3,20]{1,0:T(4,128)S(1)}, u32[]{:S(2)}, u32[]{:S(2)}) collective-permute-start(s32[3,20]{1,0:T(4,128)S(1)} %collective-permute-done), channel_id=1, source_target_pairs={{0,63},{1,0},{2,1},{3,2},{4,3},{5,4},{6,5},{7,6},{8,7},{9,8},{10,9... | collective-permute-start | bytes 728 | tf_op jit(solution)/shard_map/ppermute | solution.py:11
  115.0 6.5 %collective-permute-start.6 = (s32[3,20]{1,0:T(4,128)S(1)}, s32[3,20]{1,0:T(4,128)S(1)}, u32[]{:S(2)}, u32[]{:S(2)}) collective-permute-start(s32[3,20]{1,0:T(4,128)S(1)} %collective-permute-done.3), channel_id=1, source_target_pairs={{0,63},{1,0},{2,1},{3,2},{4,3},{5,4},{6,5},{7,6},{8,7},{9,8},{10,9... | collective-permute-start | bytes 728 | tf_op jit(solution)/shard_map/ppermute | solution.py:11
  122.3 2.4 collective-permute-start.9
  124.7 2.3 convert_bitcast_fusion.3
  127.0 3.0 fusion.41
  130.1 7.4 %collective-permute-start.11 = (bf16[1,3,20,128,128]{4,3,2,1,0:T(8,128)(2,1)S(1)}, bf16[1,3,20,128,128]{4,3,2,1,0:T(8,128)(2,1)S(1)}, u32[]{:S(2)}, u32[]{:S(2)}) collective-permute-start(bf16[1,3,20,128,128]{4,3,2,1,0:T(8,128)(2,1)S(1)} %collective-permute-done.8), channel_id=1, source_target_pairs={{0,63},{1,0},{2,1},{3,2},{4,3},{5,4},{6,5},{7,6},{8,7},{9,8},{10,9... | collective-permute-start | bytes 5898248 | tf_op jit(solution)/shard_map/ppermute | solution.py:11
  139.8 3.0 fusion.51
  145.1 3.0 fusion.61
  148.2 9.4 %collective-permute-done.11 = bf16[1,3,20,128,128]{4,3,2,1,0:T(8,128)(2,1)S(1)} collective-permute-done((bf16[1,3,20,128,128]{4,3,2,1,0:T(8,128)(2,1)S(1)}, bf16[1,3,20,128,128]{4,3,2,1,0:T(8,128)(2,1)S(1)}, u32[]{:S(2)}, u32[]{:S(2)}) %collective-permute-start.11) | collective-permute-done | bytes 1966112 | tf_op jit(solution)/shard_map/ppermute | solution.py:11
  159.8 3.0 fusion.71
  162.9 5.7 %copy.24 = f32[3,5,3,128,128]{4,2,1,0,3:T(4,128)} copy(f32[3,5,3,128,128]{3,4,2,0,1:T(8,128)} %fusion.71) | data formatting | bytes 5898240 | tf_op jit(solution)/shard_map/stack | solution.py:47
  171.2 16.0 %psum.7 = f32[384]{0:T(512)} all-reduce(f32[384]{0:T(512)S(1)} %bitcast.184), channel_id=1, replica_groups=mesh['freq'=8,'cells'=64] {'freq'}, use_global_device_ids=true, to_apply=%region_1.0 | all-reduce | flops 384 | bytes 3072 | tf_op jit(solution)/shard_map/psum | solution.py:61
  187.1 167.7 %all-reduce.3.cloned.1.call-done = f32[3,5,3,128,128]{4,2,1,0,3:T(4,128)} async-done(((f32[3,5,3,128,128]{4,2,1,0,3:T(4,128)}), f32[3,5,3,128,128]{4,2,1,0,3:T(4,128)}) %all-reduce.3.cloned.1.call-update) | async-done | bytes 2949136
  (33 shorter events, 16.3 us)
Async XLA Ops:
  7.2 161.4 %copy-start = (bf16[1,4096]{1,0:T(2,128)(2,1)S(1)}, bf16[1,4096]{1,0:T(2,128)(2,1)}, u32[]{:S(2)}) copy-start(bf16[1,4096]{1,0:T(2,128)(2,1)} %param.7) | copy-start | bytes 24580
  7.2 347.7 %all-reduce.3.cloned.1.call-start = ((), (), s32[]{:S(2)}) async-start(), calls=%async_computation | async-start | bytes 7864320
  7.2 28.6 %collective-permute-start.2 = (bf16[1,3,20,128,128]{4,3,2,1,0:T(8,128)(2,1)}, bf16[1,3,20,128,128]{4,3,2,1,0:T(8,128)(2,1)S(1)}, u32[]{:S(2)}, u32[]{:S(2)}) collective-permute-start(bf16[1,3,20,128,128]{4,3,2,1,0:T(8,128)(2,1)} %param.4), channel_id=1, source_target_pairs={{0,63},{1,0},{2,1},{3,2},{4,3},{5,4},{6,5},{7,6},{8,7},{9,8},{10,9... | collective-permute-start | bytes 5898248 | tf_op jit(solution)/shard_map/ppermute | solution.py:11
  35.8 27.4 %collective-permute-start.5 = (bf16[1,3,20,128,128]{4,3,2,1,0:T(8,128)(2,1)S(1)}, bf16[1,3,20,128,128]{4,3,2,1,0:T(8,128)(2,1)S(1)}, u32[]{:S(2)}, u32[]{:S(2)}) collective-permute-start(bf16[1,3,20,128,128]{4,3,2,1,0:T(8,128)(2,1)S(1)} %collective-permute-done.2), channel_id=1, source_target_pairs={{0,63},{1,0},{2,1},{3,2},{4,3},{5,4},{6,5},{7,6},{8,7},{9,8},{10,9... | collective-permute-start | bytes 5898248 | tf_op jit(solution)/shard_map/ppermute | solution.py:11
  46.4 59.1 %collective-permute-start = (s32[3,20]{1,0:T(4,128)}, s32[3,20]{1,0:T(4,128)S(1)}, u32[]{:S(2)}, u32[]{:S(2)}) collective-permute-start(s32[3,20]{1,0:T(4,128)} %param.5), channel_id=1, source_target_pairs={{0,63},{1,0},{2,1},{3,2},{4,3},{5,4},{6,5},{7,6},{8,7},{9,8},{10,9... | collective-permute-start | bytes 728 | tf_op jit(solution)/shard_map/ppermute | solution.py:11
  53.7 25.2 %collective-permute-start.1 = (s32[3]{0:T(128)}, s32[3]{0:T(128)S(1)}, u32[]{:S(2)}, u32[]{:S(2)}) collective-permute-start(s32[3]{0:T(128)} %param.6), channel_id=1, source_target_pairs={{0,63},{1,0},{2,1},{3,2},{4,3},{5,4},{6,5},{7,6},{8,7},{9,8},{10,9... | collective-permute-start | bytes 44 | tf_op jit(solution)/shard_map/ppermute | solution.py:11
  56.4 19.5 %copy-start.1 = (bf16[1,3,20,128,128]{4,3,2,1,0:T(8,128)(2,1)S(1)}, bf16[1,3,20,128,128]{4,3,2,1,0:T(8,128)(2,1)}, u32[]{:S(2)}) copy-start(bf16[1,3,20,128,128]{4,3,2,1,0:T(8,128)(2,1)} %param.4) | copy-start | bytes 5898244
  60.4 64.3 %copy-start.2 = (s32[3,20]{1,0:T(4,128)S(1)}, s32[3,20]{1,0:T(4,128)}, u32[]{:S(2)}) copy-start(s32[3,20]{1,0:T(4,128)} %param.5) | copy-start | bytes 724
  63.2 66.8 %collective-permute-start.8 = (bf16[1,3,20,128,128]{4,3,2,1,0:T(8,128)(2,1)S(1)}, bf16[1,3,20,128,128]{4,3,2,1,0:T(8,128)(2,1)S(1)}, u32[]{:S(2)}, u32[]{:S(2)}) collective-permute-start(bf16[1,3,20,128,128]{4,3,2,1,0:T(8,128)(2,1)S(1)} %collective-permute-done.5), channel_id=1, source_target_pairs={{0,63},{1,0},{2,1},{3,2},{4,3},{5,4},{6,5},{7,6},{8,7},{9,8},{10,9... | collective-permute-start | bytes 5898248 | tf_op jit(solution)/shard_map/ppermute | solution.py:11
  78.9 11.9 %collective-permute-start.4 = (s32[3]{0:T(128)S(1)}, s32[3]{0:T(128)S(1)}, u32[]{:S(2)}, u32[]{:S(2)}) collective-permute-start(s32[3]{0:T(128)S(1)} %collective-permute-done.1), channel_id=1, source_target_pairs={{0,63},{1,0},{2,1},{3,2},{4,3},{5,4},{6,5},{7,6},{8,7},{9,8},{10,9... | collective-permute-start | bytes 44 | tf_op jit(solution)/shard_map/ppermute | solution.py:11
  90.8 22.2 %collective-permute-start.7 = (s32[3]{0:T(128)S(1)}, s32[3]{0:T(128)S(1)}, u32[]{:S(2)}, u32[]{:S(2)}) collective-permute-start(s32[3]{0:T(128)S(1)} %collective-permute-done.4), channel_id=1, source_target_pairs={{0,63},{1,0},{2,1},{3,2},{4,3},{5,4},{6,5},{7,6},{8,7},{9,8},{10,9... | collective-permute-start | bytes 44 | tf_op jit(solution)/shard_map/ppermute | solution.py:11
  105.5 9.5 %collective-permute-start.3 = (s32[3,20]{1,0:T(4,128)S(1)}, s32[3,20]{1,0:T(4,128)S(1)}, u32[]{:S(2)}, u32[]{:S(2)}) collective-permute-start(s32[3,20]{1,0:T(4,128)S(1)} %collective-permute-done), channel_id=1, source_target_pairs={{0,63},{1,0},{2,1},{3,2},{4,3},{5,4},{6,5},{7,6},{8,7},{9,8},{10,9... | collective-permute-start | bytes 728 | tf_op jit(solution)/shard_map/ppermute | solution.py:11
  113.1 8.5 %collective-permute-start.10 = (s32[3]{0:T(128)S(1)}, s32[3]{0:T(128)S(1)}, u32[]{:S(2)}, u32[]{:S(2)}) collective-permute-start(s32[3]{0:T(128)S(1)} %collective-permute-done.7), channel_id=1, source_target_pairs={{0,63},{1,0},{2,1},{3,2},{4,3},{5,4},{6,5},{7,6},{8,7},{9,8},{10,9... | collective-permute-start | bytes 44 | tf_op jit(solution)/shard_map/ppermute | solution.py:11
  115.0 7.3 %collective-permute-start.6 = (s32[3,20]{1,0:T(4,128)S(1)}, s32[3,20]{1,0:T(4,128)S(1)}, u32[]{:S(2)}, u32[]{:S(2)}) collective-permute-start(s32[3,20]{1,0:T(4,128)S(1)} %collective-permute-done.3), channel_id=1, source_target_pairs={{0,63},{1,0},{2,1},{3,2},{4,3},{5,4},{6,5},{7,6},{8,7},{9,8},{10,9... | collective-permute-start | bytes 728 | tf_op jit(solution)/shard_map/ppermute | solution.py:11
  122.3 25.9 %collective-permute-start.9 = (s32[3,20]{1,0:T(4,128)S(1)}, s32[3,20]{1,0:T(4,128)S(1)}, u32[]{:S(2)}, u32[]{:S(2)}) collective-permute-start(s32[3,20]{1,0:T(4,128)S(1)} %collective-permute-done.6), channel_id=1, source_target_pairs={{0,63},{1,0},{2,1},{3,2},{4,3},{5,4},{6,5},{7,6},{8,7},{9,8},{10,9... | collective-permute-start | bytes 728 | tf_op jit(solution)/shard_map/ppermute | solution.py:11
  130.1 27.4 %collective-permute-start.11 = (bf16[1,3,20,128,128]{4,3,2,1,0:T(8,128)(2,1)S(1)}, bf16[1,3,20,128,128]{4,3,2,1,0:T(8,128)(2,1)S(1)}, u32[]{:S(2)}, u32[]{:S(2)}) collective-permute-start(bf16[1,3,20,128,128]{4,3,2,1,0:T(8,128)(2,1)S(1)} %collective-permute-done.8), channel_id=1, source_target_pairs={{0,63},{1,0},{2,1},{3,2},{4,3},{5,4},{6,5},{7,6},{8,7},{9,8},{10,9... | collective-permute-start | bytes 5898248 | tf_op jit(solution)/shard_map/ppermute | solution.py:11
Sparse Core Ops, SparseCore 0:
  168.7 186.1 all-reduce.2
where the time goes:
time: 364 us
  waiting for transfers between devices  205 us (56%)
  starting transfers between devices  89 us (24%)
  matrix products  28.9 us (8%)
  blocking collectives  16 us (4%)
  between operations  14.9 us (4%)
  local copies, waits for them, and re-layouts  8.86 us (2%)
    unnamed x2, waiting for transfers between devices  168 us
    ppermute x12, starting transfers between devices, shifted(): return lax.ppermute(x, axis, [(i, (i + by) % size) for i in range(size)])  89 us
    ppermute x12, waiting for transfers between devices, shifted(): return lax.ppermute(x, axis, [(i, (i + by) % size) for i in range(size)])  37.1 us
    psum x1, blocking collectives, on_device(): gradient = lax.psum(grad_part, 'freq')  16 us
    dot_general x5, matrix products, panel_products(): jnp.einsum('fapij,fabpik->abjk', local_tiles, matched, preferred_element_...  15.2 us
    dot_general x5, matrix products, panel_products(): jnp.einsum('apbq,fbqik->fabpik', matches, far_tiles, preferred_element_ty...  13.1 us
  transfers between devices with their start and end apart: 13, of which 6 were waited for; matrix products, arithmetic and copies ran while one was open for 7% of the time, Pallas kernels for 0%

commit v1 on v0

v1 whole, which is shorter than its diff:
```python
import functools

import jax
import jax.numpy as jnp
from jax import lax
from jax.experimental import pallas as pl
from jax.experimental.pallas import tpu as pltpu
from jax.sharding import PartitionSpec as P

SHIFTS = 4
NY = 4
PIECES = 4
MESH = pl.DeviceIdType.MESH


def band_kernel(
    jac, tab_vmem, tab_smem, resid, band, grad,
    own, pan_r1, pan_a, pan_r2, pan_b, far_tab, far_smem,
    dense, own_t, prod, y_in, y_sum, x_in, g_own, g_in, g_sum, g_x,
    s_load, s_tab_s, s_tab_r, s_tab_l, s_zs, s_zr, s_xs, s_xr,
    s_1s, s_1r, s_2s, s_2r, s_ys, s_yr, s_xls, s_xlr, s_gs, s_gr, s_gxs, s_gxr,
):
    blocks, slots = jac.shape[:2]
    tips = resid.shape[1] // 128
    piece = slots // PIECES
    rows = band.shape[3]
    f = lax.axis_index("freq")
    d = lax.axis_index("cells")
    nf = lax.axis_size("freq")
    nd = lax.axis_size("cells")
    y, xl = f // 2, lax.rem(f, 2)
    hi, core = lax.rem(d // 2, 2), lax.rem(d, 2)

    def cell(k):
        return (f, lax.rem(d + k + nd, nd))

    def ydev(dy):
        return (lax.rem(f + 2 * dy, nf), d)

    x_pair = (f, d + 2 - 4 * hi)
    core_pair = (f, d + 1 - 2 * core)
    xl_pair = (f + 1 - 2 * xl, d)

    loads = []
    for b in range(blocks):
        cp = pltpu.make_async_copy(jac.at[b], own[b].at[pl.ds(0, slots)], s_load.at[b])
        cp.start()
        loads.append(cp)

    barrier = pltpu.get_barrier_semaphore()
    partners = [cell(k) for k in range(-SHIFTS, SHIFTS + 1) if k != 0]
    partners += [ydev(dy) for dy in range(1, NY)] + [xl_pair]
    for dev in partners:
        pl.semaphore_signal(barrier, inc=1, device_id=dev, device_id_type=MESH)
    zero = jnp.zeros((128, 128), jnp.bfloat16)
    for panel in (own, pan_r1, pan_a, pan_r2, pan_b):
        for block in panel:
            block[slots] = zero
    pl.semaphore_wait(barrier, len(partners))

    def remote(src, dst, ss, rs, dev):
        return pltpu.make_async_remote_copy(
            src_ref=src, dst_ref=dst, send_sem=ss, recv_sem=rs,
            device_id=dev, device_id_type=MESH)

    tab_copies = [
        remote(tab_vmem, far_tab.at[k - 1], s_tab_s.at[k - 1], s_tab_r.at[k - 1], cell(-k))
        for k in range(1, SHIFTS + 1)]
    for cp in tab_copies:
        cp.start()

    source = [jac.at[b] for b in range(blocks)]

    def z_copy(b, j):
        i, part = b * PIECES + j, pl.ds(j * piece, piece)
        return remote(source[b].at[part], pan_b[b].at[part], s_zs.at[i], s_zr.at[i], cell(-4))

    def x_copy(src, b, j):
        i, part = b * PIECES + j, pl.ds(j * piece, piece)
        return remote(src[b].at[part], pan_a[b].at[part], s_xs.at[i], s_xr.at[i], x_pair)

    def core_copy(src, dst, ss, rs, b):
        part = pl.ds(0, slots)
        return remote(src[b].at[part], dst[b].at[part], ss.at[b], rs.at[b], core_pair)

    for b in range(blocks):
        for j in range(PIECES):
            z_copy(b, j).start()

            @pl.when(hi == 1)
            def _():
                x_copy(source, b, j).start()

    @pl.when(core == 1)
    def _():
        for b in range(blocks):
            core_copy(source, pan_r1, s_1s, s_1r, b).start()

    for cp in loads:
        cp.wait()

    def turn(t, carry):
        at = pl.ds(pl.multiple_of(t * 128, 128), 128)
        for a in range(blocks):
            tile = own[a][tab_smem[a, t]].T
            for g in range(2 * NY):
                own_t[pl.ds((g * blocks + a) * rows, rows), at] = tile[g * rows:(g + 1) * rows]
        return carry

    lax.fori_loop(0, tips, turn, 0)

    def unit_id(k, b):
        return k * blocks + b

    def y_copy(u, dy):
        take = pl.ds(pl.multiple_of(lax.rem(y + dy, NY) * 2 * blocks * rows, 8), 2 * blocks * rows)
        i = u * (NY - 1) + dy - 1
        return remote(prod.at[u, take], y_in.at[u, dy - 1], s_ys.at[i], s_yr.at[i], ydev(dy))

    def xl_copy(u):
        give = pl.ds(pl.multiple_of((1 - xl) * blocks * rows, 8), blocks * rows)
        return remote(y_sum.at[u, give], x_in.at[u], s_xls.at[u], s_xlr.at[u], xl_pair)

    def compute(panel, table, k, b):
        def fill(t, carry):
            dense[pl.ds(pl.multiple_of(t * 128, 128), 128), :] = panel[b][table(b, t)]
            return carry

        lax.fori_loop(0, tips, fill, 0)
        u = unit_id(k, b)
        prod[u] = jnp.dot(own_t[...], dense[...], preferred_element_type=jnp.float32)
        for dy in range(1, NY):
            y_copy(u, dy).start()

    def y_finish(u):
        for dy in range(1, NY):
            y_copy(u, dy).wait_recv()
        mine = pl.ds(pl.multiple_of(y * 2 * blocks * rows, 8), 2 * blocks * rows)
        y_sum[u] = prod[u, mine] + y_in[u, 0] + y_in[u, 1] + y_in[u, 2]
        xl_copy(u).start()

    def x_finish(u):
        xl_copy(u).wait_recv()
        keep = pl.ds(pl.multiple_of(xl * blocks * rows, 8), blocks * rows)
        k, b = u // blocks, u % blocks
        total = y_sum[u, keep] + x_in[u]
        for a in range(blocks):
            band[a, k, b] = total[a * rows:(a + 1) * rows]

    queue = []

    def advance(lag_y, lag_x):
        while len(queue) - advance.y > lag_y:
            y_finish(queue[advance.y])
            advance.y += 1
        while advance.y - advance.x > lag_x:
            x_finish(queue[advance.x])
            advance.x += 1

    advance.y = 0
    advance.x = 0

    r = jnp.broadcast_to(resid[...], (16, resid.shape[1]))
    for b in range(blocks):
        compute(own, lambda b, t: tab_smem[b, t], 0, b)
        queue.append(unit_id(0, b))
        g_own[:, pl.ds(b * 128, 128)] = jnp.dot(
            r, dense[...], preferred_element_type=jnp.float32)[:8]

    def g_copy(dy):
        return remote(g_own, g_in.at[y], s_gs.at[dy - 1], s_gr.at[dy - 1], ydev(dy))

    def g_recv(dy):
        return remote(g_own, g_in.at[lax.rem(y - dy + NY, NY)], s_gs.at[dy - 1], s_gr.at[dy - 1], ydev(dy))

    for dy in range(1, NY):
        g_copy(dy).start()
    g_in[y] = g_own[...]

    for k in range(1, SHIFTS + 1):
        tab_copies[k - 1].wait_recv()
        pltpu.make_async_copy(far_tab.at[k - 1], far_smem.at[k - 1], s_tab_l.at[k - 1]).start()
    for k in range(1, SHIFTS + 1):
        pltpu.make_async_copy(far_tab.at[k - 1], far_smem.at[k - 1], s_tab_l.at[k - 1]).wait()

    for dy in range(1, NY):
        g_recv(dy).wait_recv()
    g_sum[...] = ((g_in[0] + g_in[1]) + g_in[2]) + g_in[3]
    gx_copy = remote(g_sum, g_x, s_gxs.at[0], s_gxr.at[0], xl_pair)
    gx_copy.start()

    far = lambda k: (lambda b, t: far_smem[k - 1, b, t])
    for b in range(blocks):
        for j in range(PIECES):
            z_copy(b, j).wait_recv()

            @pl.when(hi == 0)
            def _():
                x_copy(pan_b, b, j).start()

        @pl.when(core == 0)
        def _():
            core_copy(pan_b, pan_r2, s_2s, s_2r, b).start()

        compute(pan_b, far(4), 4, b)
        queue.append(unit_id(4, b))
        advance(2, 2)
        for j in range(PIECES):
            x_copy(source, b, j).wait_recv()

        @pl.when(core == 0)
        def _():
            core_copy(pan_a, pan_r1, s_1s, s_1r, b).start()

        @pl.when(core == 1)
        def _():
            core_copy(pan_a, pan_r2, s_2s, s_2r, b).start()

        compute(pan_a, far(2), 2, b)
        queue.append(unit_id(2, b))
        advance(2, 2)
        core_copy(source, pan_r1, s_1s, s_1r, b).wait_recv()
        compute(pan_r1, far(1), 1, b)
        queue.append(unit_id(1, b))
        advance(2, 2)
        core_copy(source, pan_r2, s_2s, s_2r, b).wait_recv()
        compute(pan_r2, far(3), 3, b)
        queue.append(unit_id(3, b))
        advance(2, 2)

    gx_copy.wait_recv()
    grad[...] = (g_sum[...] + g_x[...])[:1]
    advance(1, 1)
    advance(0, 0)

    for cp in tab_copies:
        cp.wait_send()
    for b in range(blocks):
        for j in range(PIECES):
            z_copy(b, j).wait_send()
            x_copy(source, b, j).wait_send()
        core_copy(source, pan_r1, s_1s, s_1r, b).wait_send()
        core_copy(source, pan_r2, s_2s, s_2r, b).wait_send()
    for u in range(blocks * (SHIFTS + 1)):
        for dy in range(1, NY):
            y_copy(u, dy).wait_send()
        xl_copy(u).wait_send()
    for dy in range(1, NY):
        g_copy(dy).wait_send()
    gx_copy.wait_send()


def on_device(jacobian_tiles, tip_lists, counts, residual):
    _, blocks, slots, tile, _ = jacobian_tiles.shape
    tips = residual.shape[1] // tile
    nf = lax.axis_size("freq")
    rows = tile // nf
    units = blocks * (SHIFTS + 1)
    width = blocks * tile
    slot_ids = jnp.arange(slots, dtype=jnp.int32)
    live = slot_ids[None, :] < counts[:, None]
    tip_ids = jnp.arange(128, dtype=jnp.int32)
    hit = (tip_lists[:, :, None] == tip_ids[None, None, :]) & live[:, :, None]
    table = jnp.min(jnp.where(hit, slot_ids[None, :, None], slots), axis=1)
    table = jnp.pad(table, ((0, 8 - blocks), (0, 0)))
    dma = pltpu.SemaphoreType.DMA
    bf16, f32 = jnp.bfloat16, jnp.float32
    vm = pltpu.VMEM
    panel = [vm((slots + 1, tile, tile), bf16)] * blocks
    pieces = blocks * PIECES
    band, grad = pl.pallas_call(
        band_kernel,
        out_shape=(
            jax.ShapeDtypeStruct((blocks, SHIFTS + 1, blocks, rows, tile), f32),
            jax.ShapeDtypeStruct((1, width), f32),
        ),
        in_specs=[
            pl.BlockSpec(memory_space=pl.ANY),
            pl.BlockSpec(memory_space=pltpu.VMEM),
            pl.BlockSpec(memory_space=pltpu.SMEM),
            pl.BlockSpec(memory_space=pltpu.VMEM),
        ],
        out_specs=(pl.BlockSpec(memory_space=pltpu.VMEM), pl.BlockSpec(memory_space=pltpu.VMEM)),
        scratch_shapes=[
            panel, panel, panel, panel, panel,
            vm((SHIFTS, 8, 128), jnp.int32), pltpu.SMEM((SHIFTS, 8, 128), jnp.int32),
            vm((tips * tile, tile), bf16), vm((width, tips * tile), bf16),
            vm((units, width, tile), f32), vm((units, NY - 1, width // NY, tile), f32),
            vm((units, width // NY, tile), f32), vm((units, width // nf, tile), f32),
            vm((8, width), f32), vm((NY, 8, width), f32), vm((8, width), f32), vm((8, width), f32),
            dma((blocks,)), dma((SHIFTS,)), dma((SHIFTS,)), dma((SHIFTS,)),
            dma((pieces,)), dma((pieces,)), dma((pieces,)), dma((pieces,)),
            dma((blocks,)), dma((blocks,)), dma((blocks,)), dma((blocks,)),
            dma((units * (NY - 1),)), dma((units * (NY - 1),)), dma((units,)), dma((units,)),
            dma((NY - 1,)), dma((NY - 1,)), dma((1,)), dma((1,)),
        ],
        compiler_params=pltpu.CompilerParams(
            collective_id=0, has_side_effects=True, vmem_limit_bytes=48 * 1024 * 1024),
    )(jacobian_tiles.reshape(blocks, slots, tile, tile), table, table, residual)
    return band, grad.reshape(width)


def solution(mesh):
    placed = (P("freq", "cells", None, None, None), P("cells", None), P("cells"), P("freq", None))
    return jax.shard_map(
        on_device,
        mesh=mesh,
        in_specs=placed,
        out_specs=(P("cells", None, None, "freq", None), P("cells")),
        check_vma=False,
    )
```

time: 364 us -> 105 us (0.29)
  the two profiles are of different devices: /device:TPU:1 before, /device:TPU:4 now
where the time goes in v1:
time: 105 us; the launch traced here: 104 us
  Pallas kernels  98.7 us (94%)
  local copies, waits for them, and re-layouts  3 us (3%)
  other arithmetic  2.1 us (2%)
    pallas_call x1, Pallas kernels, on_device(): pl.pallas_call(band_kernel, out_shape=(jax.ShapeDtypeStruct((blocks, SHIF...  98.7 us
    unnamed x5, local copies, waits for them, and re-layouts  2.99 us

profile of v1, /device:TPU:4, one launch (start us, length us, event | category | flops | bytes accessed | tf_op | source)
XLA Modules:
  0.0 104.5 jit_solution(1959377265767139127)
XLA Ops:
  0.6 0.7 iota_compare_fusion.1
  1.4 0.8 select_reduce_fusion
  2.2 0.0 copy-start
  2.2 1.5 %copy-done = bf16[1,3,20,128,128]{4,3,2,1,0:T(8,128)(2,1)S(1)} copy-done((bf16[1,3,20,128,128]{4,3,2,1,0:T(8,128)(2,1)S(1)}, bf16[1,3,20,128,128]{4,3,2,1,0:T(8,128)(2,1)}, u32[]{:S(2)}) %copy-start) | copy-done | bytes 1966104
  3.7 0.0 copy-start.1
  3.7 0.7 copy-done.1
  4.4 98.7 %shard_map.59 = (f32[3,5,3,16,128]{4,3,2,1,0:T(8,128)S(1)}, f32[1,384]{1,0:T(1,128)S(1)}) custom-call(bf16[3,20,128,128]{3,2,1,0:T(8,128)(2,1)S(1)} %bitcast.1, s32[8,128]{1,0:T(8,128)S(1)} %pad.4.tab_vmem.tab_smem, s32[8,128]{1,0:T(8,128)S(1)} %pad.4.tab_vmem.tab_smem, bf16[1,4096]{1,0:T(2,128)(2,1)S(1)} %copy-done.1), custom_call_target="tpu_custom_call" | custom-call | tf_op jit(solution)/shard_map/pallas_call | solution.py:271
  103.1 0.6 reduce
  103.7 0.7 copy.7
  (1 shorter events, 0.0 us)
Async XLA Ops:
  2.2 1.5 %copy-start = (bf16[1,3,20,128,128]{4,3,2,1,0:T(8,128)(2,1)S(1)}, bf16[1,3,20,128,128]{4,3,2,1,0:T(8,128)(2,1)}, u32[]{:S(2)}) copy-start(bf16[1,3,20,128,128]{4,3,2,1,0:T(8,128)(2,1)} %param.4) | copy-start | bytes 5898244
  3.7 0.7 copy-start.1

commit v2 on v1

--- a/solution.py
+++ b/solution.py
@@ -14,14 +14,14 @@
 
 
 def band_kernel(
-    jac, tab_vmem, tab_smem, resid, band, grad,
-    own, pan_r1, pan_a, pan_r2, pan_b, far_tab, far_smem,
+    jac, tip_lists, counts, resid_hbm, band, grad,
+    own, pan_r1, pan_a, pan_r2, pan_b, resid, tab_vmem, tab_smem, far_tab, far_smem,
     dense, own_t, prod, y_in, y_sum, x_in, g_own, g_in, g_sum, g_x,
-    s_load, s_tab_s, s_tab_r, s_tab_l, s_zs, s_zr, s_xs, s_xr,
+    s_load, s_own_tab, s_tab_s, s_tab_r, s_tab_l, s_zs, s_zr, s_xs, s_xr,
     s_1s, s_1r, s_2s, s_2r, s_ys, s_yr, s_xls, s_xlr, s_gs, s_gr, s_gxs, s_gxr,
 ):
     blocks, slots = jac.shape[:2]
-    tips = resid.shape[1] // 128
+    tips = resid_hbm.shape[1] // 128
     piece = slots // PIECES
     rows = band.shape[3]
     f = lax.axis_index("freq")
@@ -47,11 +47,24 @@
         cp.start()
         loads.append(cp)
 
+    resid_load = pltpu.make_async_copy(resid_hbm, resid, s_load.at[blocks])
+    resid_load.start()
+
     barrier = pltpu.get_barrier_semaphore()
     partners = [cell(k) for k in range(-SHIFTS, SHIFTS + 1) if k != 0]
     partners += [ydev(dy) for dy in range(1, NY)] + [xl_pair]
     for dev in partners:
         pl.semaphore_signal(barrier, inc=1, device_id=dev, device_id_type=MESH)
+    row = lax.broadcasted_iota(jnp.int32, (8, 128), 0)
+    tip = lax.broadcasted_iota(jnp.int32, (8, 128), 1)
+    table = jnp.full((8, 128), slots, jnp.int32)
+    for b in range(blocks):
+        for p in range(slots):
+            named = jnp.where(p < counts[b], tip_lists[b, p], -1)
+            table = jnp.where((row == b) & (tip == named), p, table)
+    tab_vmem[...] = table
+    own_tab = pltpu.make_async_copy(tab_vmem, tab_smem, s_own_tab.at[0])
+    own_tab.start()
     zero = jnp.zeros((128, 128), jnp.bfloat16)
     for panel in (own, pan_r1, pan_a, pan_r2, pan_b):
         for block in panel:
@@ -98,6 +111,9 @@
 
     for cp in loads:
         cp.wait()
+    resid_load.wait()
+    own_tab.wait()
+    own_t[pl.ds(blocks * 128, 16), :] = jnp.broadcast_to(resid[...], (16, tips * 128))
 
     def turn(t, carry):
         at = pl.ds(pl.multiple_of(t * 128, 128), 128)
@@ -107,7 +123,9 @@
                 own_t[pl.ds((g * blocks + a) * rows, rows), at] = tile[g * rows:(g + 1) * rows]
         return carry
 
-    lax.fori_loop(0, tips, turn, 0)
+    lax.fori_loop(0, tips, turn, 0, unroll=2)
+
+    queue = []
 
     def unit_id(k, b):
         return k * blocks + b
@@ -121,16 +139,31 @@
         give = pl.ds(pl.multiple_of((1 - xl) * blocks * rows, 8), blocks * rows)
         return remote(y_sum.at[u, give], x_in.at[u], s_xls.at[u], s_xlr.at[u], xl_pair)
 
-    def compute(panel, table, k, b):
-        def fill(t, carry):
-            dense[pl.ds(pl.multiple_of(t * 128, 128), 128), :] = panel[b][table(b, t)]
+    def fill(panel, table, b, column):
+        at = pl.ds(column * 128, 128)
+
+        def step(t, carry):
+            dense[pl.ds(pl.multiple_of(t * 128, 128), 128), at] = panel[b][table(b, t)]
             return carry
 
-        lax.fori_loop(0, tips, fill, 0)
-        u = unit_id(k, b)
-        prod[u] = jnp.dot(own_t[...], dense[...], preferred_element_type=jnp.float32)
+        lax.fori_loop(0, tips, step, 0, unroll=4)
+
+    def send(u):
         for dy in range(1, NY):
             y_copy(u, dy).start()
+        queue.append(u)
+
+    def pair(first, second):
+        both = []
+        for column, (panel, table, k, b) in enumerate((first, second)):
+            fill(panel, table, b, column)
+            both.append(unit_id(k, b))
+        width = blocks * 128
+        out = jnp.dot(own_t[pl.ds(0, width), :], dense[:, pl.ds(0, 256)],
+                      preferred_element_type=jnp.float32)
+        for column, u in enumerate(both):
+            prod[u] = out[:, column * 128:(column + 1) * 128]
+            send(u)
 
     def y_finish(u):
         for dy in range(1, NY):
@@ -147,8 +180,6 @@
         for a in range(blocks):
             band[a, k, b] = total[a * rows:(a + 1) * rows]
 
-    queue = []
-
     def advance(lag_y, lag_x):
         while len(queue) - advance.y > lag_y:
             y_finish(queue[advance.y])
@@ -160,12 +191,13 @@
     advance.y = 0
     advance.x = 0
 
-    r = jnp.broadcast_to(resid[...], (16, resid.shape[1]))
-    for b in range(blocks):
-        compute(own, lambda b, t: tab_smem[b, t], 0, b)
-        queue.append(unit_id(0, b))
-        g_own[:, pl.ds(b * 128, 128)] = jnp.dot(
-            r, dense[...], preferred_element_type=jnp.float32)[:8]
+    for b in range(blocks):
+        fill(own, lambda b, t: tab_smem[b, t], b, b)
+    out = jnp.dot(own_t[...], dense[...], preferred_element_type=jnp.float32)
+    for b in range(blocks):
+        prod[unit_id(0, b)] = out[:blocks * 128, b * 128:(b + 1) * 128]
+        send(unit_id(0, b))
+    g_own[...] = out[blocks * 128:blocks * 128 + 8]
 
     def g_copy(dy):
         return remote(g_own, g_in.at[y], s_gs.at[dy - 1], s_gr.at[dy - 1], ydev(dy))
@@ -202,9 +234,6 @@
         def _():
             core_copy(pan_b, pan_r2, s_2s, s_2r, b).start()
 
-        compute(pan_b, far(4), 4, b)
-        queue.append(unit_id(4, b))
-        advance(2, 2)
         for j in range(PIECES):
             x_copy(source, b, j).wait_recv()
 
@@ -216,20 +245,17 @@
         def _():
             core_copy(pan_a, pan_r2, s_2s, s_2r, b).start()
 
-        compute(pan_a, far(2), 2, b)
-        queue.append(unit_id(2, b))
+        pair((pan_b, far(4), 4, b), (pan_a, far(2), 2, b))
         advance(2, 2)
         core_copy(source, pan_r1, s_1s, s_1r, b).wait_recv()
-        compute(pan_r1, far(1), 1, b)
-        queue.append(unit_id(1, b))
+        core_copy(source, pan_r2, s_2s, s_2r, b).wait_recv()
+        pair((pan_r1, far(1), 1, b), (pan_r2, far(3), 3, b))
         advance(2, 2)
-        core_copy(source, pan_r2, s_2s, s_2r, b).wait_recv()
-        compute(pan_r2, far(3), 3, b)
-        queue.append(unit_id(3, b))
-        advance(2, 2)
 
     gx_copy.wait_recv()
-    grad[...] = (g_sum[...] + g_x[...])[:1]
+    for b in range(blocks):
+        at = pl.ds(b * 128, 128)
+        grad[pl.ds(b, 1), :] = g_sum[pl.ds(0, 1), at] + g_x[pl.ds(0, 1), at]
     advance(1, 1)
     advance(0, 0)
 
@@ -257,12 +283,6 @@
     rows = tile // nf
     units = blocks * (SHIFTS + 1)
     width = blocks * tile
-    slot_ids = jnp.arange(slots, dtype=jnp.int32)
-    live = slot_ids[None, :] < counts[:, None]
-    tip_ids = jnp.arange(128, dtype=jnp.int32)
-    hit = (tip_lists[:, :, None] == tip_ids[None, None, :]) & live[:, :, None]
-    table = jnp.min(jnp.where(hit, slot_ids[None, :, None], slots), axis=1)
-    table = jnp.pad(table, ((0, 8 - blocks), (0, 0)))
     dma = pltpu.SemaphoreType.DMA
     bf16, f32 = jnp.bfloat16, jnp.float32
     vm = pltpu.VMEM
@@ -272,31 +292,32 @@
         band_kernel,
         out_shape=(
             jax.ShapeDtypeStruct((blocks, SHIFTS + 1, blocks, rows, tile), f32),
-            jax.ShapeDtypeStruct((1, width), f32),
+            jax.ShapeDtypeStruct((blocks, tile), f32),
         ),
         in_specs=[
-            pl.BlockSpec(memory_space=pl.ANY),
-            pl.BlockSpec(memory_space=pltpu.VMEM),
+            pl.BlockSpec(memory_space=pltpu.HBM),
             pl.BlockSpec(memory_space=pltpu.SMEM),
-            pl.BlockSpec(memory_space=pltpu.VMEM),
+            pl.BlockSpec(memory_space=pltpu.SMEM),
+            pl.BlockSpec(memory_space=pltpu.HBM),
         ],
         out_specs=(pl.BlockSpec(memory_space=pltpu.VMEM), pl.BlockSpec(memory_space=pltpu.VMEM)),
         scratch_shapes=[
             panel, panel, panel, panel, panel,
+            vm((1, tips * tile), bf16), vm((8, 128), jnp.int32), pltpu.SMEM((8, 128), jnp.int32),
             vm((SHIFTS, 8, 128), jnp.int32), pltpu.SMEM((SHIFTS, 8, 128), jnp.int32),
-            vm((tips * tile, tile), bf16), vm((width, tips * tile), bf16),
+            vm((tips * tile, width), bf16), vm((width + 16, tips * tile), bf16),
             vm((units, width, tile), f32), vm((units, NY - 1, width // NY, tile), f32),
             vm((units, width // NY, tile), f32), vm((units, width // nf, tile), f32),
             vm((8, width), f32), vm((NY, 8, width), f32), vm((8, width), f32), vm((8, width), f32),
-            dma((blocks,)), dma((SHIFTS,)), dma((SHIFTS,)), dma((SHIFTS,)),
+            dma((blocks + 1,)), dma((1,)), dma((SHIFTS,)), dma((SHIFTS,)), dma((SHIFTS,)),
             dma((pieces,)), dma((pieces,)), dma((pieces,)), dma((pieces,)),
             dma((blocks,)), dma((blocks,)), dma((blocks,)), dma((blocks,)),
             dma((units * (NY - 1),)), dma((units * (NY - 1),)), dma((units,)), dma((units,)),
             dma((NY - 1,)), dma((NY - 1,)), dma((1,)), dma((1,)),
         ],
         compiler_params=pltpu.CompilerParams(
-            collective_id=0, has_side_effects=True, vmem_limit_bytes=48 * 1024 * 1024),
-    )(jacobian_tiles.reshape(blocks, slots, tile, tile), table, table, residual)
+            collective_id=0, has_side_effects=True, vmem_limit_bytes=63 * 1024 * 1024),
+    )(jacobian_tiles.reshape(blocks, slots, tile, tile), tip_lists, counts, residual)
     return band, grad.reshape(width)
 
 

time: 105 us -> 102 us (0.971)
  other arithmetic: 2.1 us -> 0 us
    unnamed x5 -> x2, local copies, waits for them, and re-layouts: 2.99 us -> 3 us
where the time goes in v2:
time: 102 us
  Pallas kernels  98.6 us (97%)
  local copies, waits for them, and re-layouts  3 us (3%)
    pallas_call x1, Pallas kernels, on_device(): pl.pallas_call(band_kernel, out_shape=(jax.ShapeDtypeStruct((blocks, SHIF...  98.6 us
    unnamed x2, local copies, waits for them, and re-layouts  3 us

profile of v2, /device:TPU:4, one launch (start us, length us, event | category | flops | bytes accessed | tf_op | source)
XLA Modules:
  0.0 102.2 jit_solution(5025383288727517110)
XLA Ops:
  0.6 98.6 %shard_map.59 = (f32[3,5,3,16,128]{4,3,2,1,0:T(8,128)}, f32[3,128]{1,0:T(4,128)}) custom-call(bf16[3,20,128,128]{3,2,1,0:T(8,128)(2,1)} %bitcast.2, s32[3,20]{1,0:T(4,128)} %tip_lists.1, s32[3]{0:T(128)} %counts.1, bf16[1,4096]{1,0:T(2,128)(2,1)} %resid_hbm.1), custom_call_target="tpu_custom_call" | custom-call | tf_op jit(solution)/shard_map/pallas_call | solution.py:291
  99.2 1.8 %copy.8 = f32[3,5,3,16,128]{4,3,2,1,0:T(8,128)} copy(f32[3,5,3,16,128]{4,3,2,1,0:T(8,128)} %get-tuple-element.8) | data formatting | bytes 737280
  100.9 1.2 %copy.9 = f32[384]{0:T(512)} copy(f32[384]{0:T(512)} %bitcast.3) | data formatting | bytes 3072

commit v3 on v0

v3 whole, which is shorter than its diff:
```python
import jax
import jax.numpy as jnp
from jax import lax
from jax.experimental import pallas as pl
from jax.experimental.pallas import tpu as pltpu
from jax.sharding import PartitionSpec as P

SHIFTS = 4
NY = 4
NB = 3
SCALE_ROWS = 16
MESH = pl.DeviceIdType.MESH


def unit_list():
    units = [
        ("own", None, -1, [(a, 0, b) for b in range(NB) for a in range(NB)]),
        ("mate", 0, -1, [(a, 1, b) for b in range(NB) for a in range(NB)]),
    ]
    for s in range(NB):
        grid = [(a, lane, s) for a in range(s + 1) for lane in range(2)]
        grid += [(s, lane, b) for b in range(s) for lane in range(2)]
        units.append(("side", None, s, grid))
        units.append(("cross", None, s, grid))
        for lane in range(2):
            down = [(a, lane, s) for a in range(NB)]
            up = [(s, lane, b) for b in range(NB)]
            units.append(("z", 1 if lane else None, s, down + up))
    return units


UNITS = unit_list()
COUNT = [len(blocks) for _, _, _, blocks in UNITS]
BASE = [sum(COUNT[:u]) for u in range(len(UNITS))]
TOTAL = sum(COUNT)


def band_kernel(
    jac, tip_lists, counts, resid_hbm, band, grad,
    raw, pk0, pk1, mate0, mate1, pan_d, pan_od, pan_u, pan_a, pan_oa,
    resid, tab, tab_smem, far_tab, far_smem, mate_tab, mate_smem,
    dense, left, odd_t, cross_t, prod, coded, y_in, y_sum, x_in, fin_out, fin_in,
    g_own, g_in, g_sum, g_x,
    s_load, s_ts, s_tr, s_tl, s_ds, s_dr, s_us, s_ur, s_as, s_ar, s_ms, s_mr,
    s_ods, s_odr, s_oas, s_oar, s_ys, s_yr, s_xls, s_xlr, s_fs, s_fr, s_gs, s_gr,
):
    slots = jac.shape[1]
    half = slots // 2
    pairs = resid_hbm.shape[1] // 256
    rows = band.shape[3]
    f = lax.axis_index("freq")
    d = lax.axis_index("cells")
    nf = lax.axis_size("freq")
    nd = lax.axis_size("cells")
    y, xl = f // 2, lax.rem(f, 2)
    hi, core = lax.rem(d // 2, 2), lax.rem(d, 2)

    def ydev(dy):
        return (lax.rem(f + 2 * dy, nf), d)

    below = (f, lax.rem(d - 4 + nd, nd))
    above = (f, lax.rem(d + 4, nd))
    x_pair = (f, d + 2 - 4 * hi)
    core_pair = (f, d + 1 - 2 * core)
    xl_pair = (f + 1 - 2 * xl, d)

    loads = []
    for b in range(NB):
        loads.append(pltpu.make_async_copy(jac.at[b], raw[b], s_load.at[b]))
    loads.append(pltpu.make_async_copy(resid_hbm, resid, s_load.at[NB]))
    for cp in loads:
        cp.start()

    barrier = pltpu.get_barrier_semaphore()
    partners = [below, above, x_pair, core_pair] + [ydev(dy) for dy in range(1, NY)] + [xl_pair]
    for dev in partners:
        pl.semaphore_signal(barrier, inc=1, device_id=dev, device_id_type=MESH)

    row = lax.broadcasted_iota(jnp.int32, (8, 128), 0)
    col = lax.broadcasted_iota(jnp.int32, (8, 128), 1)
    place = jnp.full((8, 128), half, jnp.int32)
    slot = jnp.zeros((8, 128), jnp.int32)
    for b in range(NB):
        odd_before = 0
        for p in range(slots):
            name = tip_lists[b, p]
            parity = lax.rem(name, 2)
            rank = jnp.where(parity == 1, odd_before, p - odd_before)
            odd_before = odd_before + parity
            mine = row == parity * 4 + b
            slot = jnp.where(mine & (col == rank), p, slot)
            named = jnp.where(p < counts[b], name // 2, -1)
            place = jnp.where(mine & (col == named), rank, place)
    tab[0] = place
    tab[1] = slot
    own_tab = pltpu.make_async_copy(tab, tab_smem, s_load.at[NB + 1])
    own_tab.start()
    zero = jnp.zeros((128, 128), jnp.bfloat16)
    for panel in (pk0, pk1, mate0, mate1, pan_d, pan_od, pan_u, pan_a, pan_oa):
        for block in panel:
            block[half] = zero
    for cp in loads:
        cp.wait()
    own_tab.wait()

    def pack(b):
        def step(i, carry):
            pk0[b][i] = raw[b][tab_smem[1, b, i]]
            pk1[b][i] = raw[b][tab_smem[1, 4 + b, i]]
            return carry

        lax.fori_loop(0, half, step, 0)

    pack(0)
    pl.semaphore_wait(barrier, len(partners))

    def remote(src, dst, ss, rs, dev):
        return pltpu.make_async_remote_copy(
            src_ref=src, dst_ref=dst, send_sem=ss, recv_sem=rs,
            device_id=dev, device_id_type=MESH)

    live = pl.ds(0, half)

    def panel_copies(src, dst, ss, rs, dev, first=0):
        return [
            remote(src[b].at[live], dst[b].at[live], ss.at[first + b], rs.at[first + b], dev)
            for b in range(NB)]

    d_copy = panel_copies(pk0, pan_d, s_ds, s_dr, below)
    u_copy = panel_copies(pk1, pan_u, s_us, s_ur, above)
    a_copy0 = panel_copies(pk0, pan_a, s_as, s_ar, x_pair)
    a_copy1 = panel_copies(pk1, pan_a, s_as, s_ar, x_pair)
    m_copy = panel_copies(pk0, mate0, s_ms, s_mr, core_pair)
    m_copy += panel_copies(pk1, mate1, s_ms, s_mr, core_pair, NB)
    od_copy = panel_copies(pan_d, pan_od, s_ods, s_odr, core_pair)
    oa_copy = panel_copies(pan_a, pan_oa, s_oas, s_oar, core_pair)
    t_copy = [
        remote(tab.at[0], far_tab.at[i], s_ts.at[i], s_tr.at[i], dev)
        for i, dev in enumerate((core_pair, below, above, x_pair))]
    mt_copy = remote(far_tab.at[pl.ds(1, 3)], mate_tab, s_ts.at[4], s_tr.at[4], core_pair)

    for b in range(NB):
        if b > 0:
            pack(b)
        d_copy[b].start()
        u_copy[b].start()

        @pl.when(hi == 1)
        def _():
            a_copy0[b].start()

        @pl.when(hi == 0)
        def _():
            a_copy1[b].start()

        if b == 0:
            for cp in t_copy:
                cp.start()
        m_copy[b].start()
        m_copy[NB + b].start()

    def turn(panel, table, b, put_tile):
        def step(t, carry):
            at = pl.ds(pl.multiple_of(t * 128, 128), 128)
            put_tile(at, panel[b][table(b, t)].T)
            return carry

        lax.fori_loop(0, pairs, step, 0, unroll=2)

    def fill(panel, table, b, which, lane):
        at = pl.ds(b * 256 + lane * 128, 128)

        def step(t, carry):
            dense[which, pl.ds(pl.multiple_of(t * 128, 128), 128), at] = panel[b][table(b, t)]
            return carry

        lax.fori_loop(0, pairs, step, 0, unroll=4)

    def own_table(parity):
        return lambda b, t: tab_smem[0, parity * 4 + b, t]

    def far_table(i, parity):
        return lambda b, t: far_smem[i, parity * 4 + b, t]

    def mate_table(i, parity):
        return lambda b, t: mate_smem[i - 1, parity * 4 + b, t]

    def put_left(which, b):
        def put(at, tile):
            left[which, pl.ds(b * 128, 128), at] = tile
        return put

    def put_odd(b):
        def put(at, tile):
            odd_t[pl.ds(b * 128, 128), at] = tile
        return put

    def put_cross(b):
        def put(at, tile):
            cross_t[pl.ds(b * 128, 128), at] = tile
        return put

    below_rows = pl.ds(NB * 128, 16)
    for t in range(pairs):
        at = pl.ds(t * 128, 128)
        left[0, below_rows, at] = jnp.broadcast_to(resid[:, pl.ds(t * 256, 128)], (16, 128))
        odd_t[below_rows, at] = jnp.broadcast_to(resid[:, pl.ds(t * 256 + 128, 128)], (16, 128))
    for b in range(NB):
        turn(pk0, own_table(0), b, put_left(0, b))
        turn(pk1, own_table(1), b, put_odd(b))
        fill(pk0, own_table(0), b, 3, 0)
        fill(pk1, own_table(1), b, 1, 0)

    for cp in t_copy:
        cp.wait_recv()
    mt_copy.start()
    far_load = pltpu.make_async_copy(far_tab, far_smem, s_tl.at[0])
    far_load.start()
    far_load.wait()

    def on(u, body):
        which = UNITS[u][1]
        if which is None:
            body()
        else:
            pl.when(core == which)(body)

    def coded_base(u):
        return BASE[u] * 128 + u * NY * SCALE_ROWS

    def y_part(u):
        return COUNT[u] * 2 * rows + SCALE_ROWS

    def y_copy(u, dy):
        part = y_part(u)
        take = pl.ds(pl.multiple_of(coded_base(u) + lax.rem(y + dy, NY) * part, 16), part)
        i = u * (NY - 1) + dy - 1
        return remote(coded.at[take], y_in.at[dy - 1, pl.ds(coded_base(u) // NY, part)],
                      s_ys.at[i], s_yr.at[i], ydev(dy))

    def xl_copy(u):
        part = rows * COUNT[u]
        give = pl.ds(pl.multiple_of(BASE[u] * 2 * rows + (1 - xl) * part, 8), part)
        return remote(y_sum.at[give], x_in.at[pl.ds(BASE[u] * rows, part)],
                      s_xls.at[u], s_xlr.at[u], xl_pair)

    def fin_copy(u):
        kind = UNITS[u][0]
        if kind == "z":
            part = pl.ds((BASE[u] + NB) * rows, rows * NB)
        else:
            part = pl.ds(BASE[u] * rows, rows * COUNT[u])
        dev = x_pair if kind == "cross" else below
        return remote(fin_out.at[part], fin_in.at[part], s_fs.at[u], s_fr.at[u], dev)

    def send(u):
        n = COUNT[u]

        def body():
            def peak(i, top):
                at = pl.ds(pl.multiple_of(BASE[u] * 128 + i * 128, 128), 128)
                return jnp.maximum(top, jnp.abs(prod[at]))

            top = lax.fori_loop(0, n, peak, jnp.zeros((128, 128), jnp.float32))
            top = jnp.full((16, 128), jnp.max(top), jnp.float32)
            power = jnp.ceil(jnp.log2(jnp.maximum(top, 1e-33)) + 1e-3)
            up = jnp.exp2(15.0 - power)[:1] * (32766.0 / 32768.0)
            for part in range(NY):
                start = coded_base(u) + part * y_part(u)

                def code(i, carry):
                    src = pl.ds(pl.multiple_of(BASE[u] * 128 + part * n * 32 + i * 32, 32), 32)
                    dst = pl.ds(pl.multiple_of(start + i * 32, 16), 32)
                    coded[dst] = jnp.round(prod[src] * up).astype(jnp.int32).astype(jnp.int16)
                    return carry

                lax.fori_loop(0, n, code, 0)
                coded[pl.ds(start + n * 32, SCALE_ROWS)] = power.astype(jnp.int32).astype(jnp.int16)
            for dy in range(1, NY):
                y_copy(u, dy).start()

        on(u, body)

    def y_finish(u):
        n = COUNT[u]

        def body():
            down = []
            for dy in range(1, NY):
                y_copy(u, dy).wait_recv()
                power = y_in[dy - 1, pl.ds(coded_base(u) // NY + n * 32, SCALE_ROWS)]
                power = power.astype(jnp.int32).astype(jnp.float32)
                down.append(jnp.exp2(power - 15.0)[:1] * (32768.0 / 32766.0))

            def step(i, carry):
                at = pl.ds(pl.multiple_of(BASE[u] * 128 + y * n * 32 + i * 32, 32), 32)
                total = prod[at]
                for dy in range(1, NY):
                    src = pl.ds(pl.multiple_of(coded_base(u) // NY + i * 32, 16), 32)
                    part = y_in[dy - 1, src].astype(jnp.int32).astype(jnp.float32)
                    total = total + part * down[dy - 1]
                y_sum[pl.ds(pl.multiple_of(BASE[u] * 32 + i * 32, 32), 32)] = total
                return carry

            lax.fori_loop(0, n, step, 0)
            xl_copy(u).start()

        on(u, body)

    def block_rows(u, i):
        return pl.ds((BASE[u] + i) * rows, rows)

    def x_finish(u):
        kind, _, _, blocks = UNITS[u]
        part = rows * COUNT[u]

        def body():
            xl_copy(u).wait_recv()
            keep = pl.ds(pl.multiple_of(BASE[u] * 2 * rows + xl * part, 8), part)
            fin_out[pl.ds(BASE[u] * rows, part)] = y_sum[keep] + x_in[pl.ds(BASE[u] * rows, part)]
            if kind == "side":
                pl.when(hi == 1)(lambda: fin_copy(u).start())
            elif kind in ("cross", "z"):
                fin_copy(u).start()

        on(u, body)

    def fin_finish(u):
        kind, _, _, blocks = UNITS[u]

        def body():
            if kind in ("own", "mate"):
                for i, (a, lane, b) in enumerate(blocks):
                    band[a, lane, b] = fin_out[block_rows(u, i)]
            elif kind == "z":
                for i, (a, lane, b) in enumerate(blocks[:NB]):
                    z_own[(a, lane, b)] = (u, i)
                fin_copy(u).wait_recv()
            elif kind == "side":
                def from_here():
                    for i, (a, lane, b) in enumerate(blocks):
                        band[a, 3 - 2 * core if lane else 2, b] = fin_out[block_rows(u, i)]

                def from_above():
                    fin_copy(u).wait_recv()
                    for i, (a, lane, b) in enumerate(blocks):
                        band[a, 3 - 2 * core if lane else 2, b] = fin_in[block_rows(u, i)]

                pl.when(hi == 0)(from_here)
                pl.when(hi == 1)(from_above)
            else:
                fin_copy(u).wait_recv()
                for i, (a, lane, b) in enumerate(blocks):
                    k = 3 - 2 * core if lane else 2
                    band[a, k, b] = band[a, k, b] + fin_in[block_rows(u, i)]

        on(u, body)

    z_own = {}

    def z_place(u):
        _, _, _, blocks = UNITS[u]

        def body():
            for i, (a, lane, b) in enumerate(blocks[NB:]):
                v, j = z_own[(a, lane, b)]
                k = 3 if lane else 4
                band[a, k, b] = fin_out[block_rows(v, j)] + fin_in[block_rows(u, NB + i)]

        on(u, body)

    def put(u, i, block):
        for g in range(2 * NY):
            at = pl.ds(BASE[u] * 128 + (g * COUNT[u] + i) * rows, rows)
            prod[at] = block[g * rows:(g + 1) * rows]

    def put_grid(u, out, rows_of, cols_of):
        for i, (a, lane, b) in enumerate(UNITS[u][3]):
            if a in rows_of and b in cols_of:
                r, c = rows_of.index(a) * 128, cols_of.index(b) * 256 + lane * 128
                put(u, i, out[r:r + 128, c:c + 128])

    def dot(a, b):
        return jnp.dot(a, b, preferred_element_type=jnp.float32)

    for b in range(NB):
        m_copy[b].wait_recv()
        m_copy[NB + b].wait_recv()
        fill(mate0, far_table(0, 0), b, 3, 1)
        fill(mate1, far_table(0, 1), b, 1, 1)
        at = pl.ds(b * 256, 256)
        out = dot(left[0], dense[3, :, at]) + dot(odd_t[...], dense[1, :, at])
        for a in range(NB):
            put(0, b * NB + a, out[a * 128:(a + 1) * 128, :128])
            put(1, b * NB + a, out[a * 128:(a + 1) * 128, 128:])
        g_own[:, pl.ds(b * 128, 128)] = out[NB * 128:NB * 128 + 8, :128]
    send(0)
    send(1)

    def g_copy(dy):
        return remote(g_own, g_in.at[y], s_gs.at[dy - 1], s_gr.at[dy - 1], ydev(dy))

    def g_recv(dy):
        return remote(g_own, g_in.at[lax.rem(y - dy + NY, NY)], s_gs.at[dy - 1], s_gr.at[dy - 1], ydev(dy))

    gx_copy = remote(g_sum, g_x, s_gs.at[NY - 1], s_gr.at[NY - 1], xl_pair)
    for dy in range(1, NY):
        g_copy(dy).start()
    g_in[y] = g_own[...]

    mt_copy.wait_recv()
    mate_load = pltpu.make_async_copy(mate_tab, mate_smem, s_tl.at[1])
    mate_load.start()
    mate_load.wait()

    def step_units(s):
        return [u for u in range(len(UNITS)) if UNITS[u][2] == s]

    for s in range(NB):
        side, cross, z_self, z_mate = step_units(s)
        d_copy[s].wait_recv()
        od_copy[s].start()
        a_copy0[s].wait_recv()
        oa_copy[s].start()

        fill(pan_d, far_table(1, 0), s, 0, 0)
        fill(pan_a, lambda b, t: far_smem[3, hi * 4 + b, t], s, 2, 0)
        turn(pan_a, lambda b, t: far_smem[3, hi * 4 + b, t], s, put_cross(s))
        u_copy[s].wait_recv()
        turn(pan_u, far_table(2, 1), s, put_left(1, s))
        od_copy[s].wait_recv()
        fill(pan_od, mate_table(1, 0), s, 0, 1)
        oa_copy[s].wait_recv()
        fill(pan_oa, lambda b, t: mate_smem[2, hi * 4 + b, t], s, 2, 1)

        upto, now = list(range(s + 1)), pl.ds(s * 256, 256)
        put_grid(cross, dot(cross_t[pl.ds(0, 128 * (s + 1)), :], dense[hi, :, now]), upto, [s])
        if s > 0:
            put_grid(cross, dot(cross_t[pl.ds(128 * s, 128), :], dense[hi, :, pl.ds(0, 256 * s)]),
                     [s], list(range(s)))
        send(cross)
        put_grid(side, dot(left[hi, pl.ds(0, 128 * (s + 1)), :], dense[2, :, now]), upto, [s])
        if s > 0:
            put_grid(side, dot(left[hi, pl.ds(128 * s, 128), :], dense[2, :, pl.ds(0, 256 * s)]),
                     [s], list(range(s)))
        send(side)
        down = dot(left[0, pl.ds(0, NB * 128), :], dense[0, :, now])
        up = dot(left[1, pl.ds(128 * s, 128), :], dense[1])
        for i in range(NB):
            for lane, u in enumerate((z_self, z_mate)):
                put(u, i, down[i * 128:(i + 1) * 128, lane * 128:(lane + 1) * 128])
                put(u, NB + i, up[:, i * 256 + lane * 128:i * 256 + (lane + 1) * 128])
        send(z_self)
        send(z_mate)
        if s == 0:
            for dy in range(1, NY):
                g_recv(dy).wait_recv()
            g_sum[...] = ((g_in[0] + g_in[1]) + g_in[2]) + g_in[3]
            gx_copy.start()
        for u in step_units(s - 1):
            y_finish(u)
        if s > 0:
            for u in step_units(s - 2):
                x_finish(u)
        if s > 1:
            for u in step_units(s - 3):
                fin_finish(u)

    gx_copy.wait_recv()
    for b in range(NB):
        at = pl.ds(b * 128, 128)
        grad[pl.ds(b, 1), :] = g_sum[pl.ds(0, 1), at] + g_x[pl.ds(0, 1), at]
    last = step_units(NB - 1)
    for u in step_units(NB - 2):
        x_finish(u)
    for u in last:
        y_finish(u)
    for u in step_units(NB - 3):
        fin_finish(u)
    for u in last:
        x_finish(u)
    for u in step_units(NB - 2) + last:
        fin_finish(u)
    for u in range(len(UNITS)):
        if UNITS[u][0] == "z":
            z_place(u)

    for cp in t_copy + [mt_copy] + d_copy + u_copy + a_copy0 + m_copy + od_copy + oa_copy:
        cp.wait_send()
    for u in range(len(UNITS)):
        kind = UNITS[u][0]

        def drain():
            for dy in range(1, NY):
                y_copy(u, dy).wait_send()
            xl_copy(u).wait_send()
            if kind == "side":
                pl.when(hi == 1)(lambda: fin_copy(u).wait_send())
            elif kind in ("cross", "z"):
                fin_copy(u).wait_send()

        on(u, drain)
    for dy in range(1, NY):
        g_copy(dy).wait_send()
    gx_copy.wait_send()


def on_device(jacobian_tiles, tip_lists, counts, residual):
    _, blocks, slots, tile, _ = jacobian_tiles.shape
    depth = residual.shape[1]
    rows = tile // lax.axis_size("freq")
    n = len(UNITS)
    width = blocks * tile
    dma = pltpu.SemaphoreType.DMA
    bf16, f32, i16, i32 = jnp.bfloat16, jnp.float32, jnp.int16, jnp.int32
    vm = pltpu.VMEM
    half = [vm((slots // 2 + 1, tile, tile), bf16)] * blocks
    coded = TOTAL * tile + n * NY * SCALE_ROWS
    per_block = [dma((blocks,))] * 2
    band, grad = pl.pallas_call(
        band_kernel,
        out_shape=(
            jax.ShapeDtypeStruct((blocks, SHIFTS + 1, blocks, rows, tile), f32),
            jax.ShapeDtypeStruct((blocks, tile), f32),
        ),
        in_specs=[
            pl.BlockSpec(memory_space=pltpu.HBM),
            pl.BlockSpec(memory_space=pltpu.SMEM),
            pl.BlockSpec(memory_space=pltpu.SMEM),
            pl.BlockSpec(memory_space=pltpu.HBM),
        ],
        out_specs=(pl.BlockSpec(memory_space=pltpu.VMEM), pl.BlockSpec(memory_space=pltpu.VMEM)),
        scratch_shapes=[
            [vm((slots, tile, tile), bf16)] * blocks, half, half, half, half, half, half, half, half, half,
            vm((1, depth), bf16), vm((2, 8, 128), i32), pltpu.SMEM((2, 8, 128), i32),
            vm((4, 8, 128), i32), pltpu.SMEM((4, 8, 128), i32),
            vm((3, 8, 128), i32), pltpu.SMEM((3, 8, 128), i32),
            vm((4, depth // 2, 2 * width), bf16), vm((2, width + 16, depth // 2), bf16),
            vm((width + 16, depth // 2), bf16), vm((width, depth // 2), bf16),
            vm((TOTAL * tile, tile), f32), vm((coded, tile), i16), vm((NY - 1, coded // NY, tile), i16),
            vm((TOTAL * 2 * rows, tile), f32), vm((TOTAL * rows, tile), f32),
            vm((TOTAL * rows, tile), f32), vm((TOTAL * rows, tile), f32),
            vm((8, width), f32), vm((NY, 8, width), f32), vm((8, width), f32), vm((8, width), f32),
            dma((blocks + 2,)), dma((5,)), dma((5,)), dma((2,)),
            *per_block, *per_block, *per_block, dma((2 * blocks,)), dma((2 * blocks,)),
            *per_block, *per_block,
            dma((n * (NY - 1),)), dma((n * (NY - 1),)), dma((n,)), dma((n,)), dma((n,)), dma((n,)),
            dma((NY,)), dma((NY,)),
        ],
        compiler_params=pltpu.CompilerParams(
            collective_id=0, has_side_effects=True, vmem_limit_bytes=63 * 1024 * 1024),
    )(jacobian_tiles.reshape(blocks, slots, tile, tile), tip_lists, counts, residual)
    return band, grad.reshape(width)


def solution(mesh):
    placed = (P("freq", "cells", None, None, None), P("cells", None), P("cells"), P("freq", None))
    return jax.shard_map(
        on_device,
        mesh=mesh,
        in_specs=placed,
        out_specs=(P("cells", None, None, "freq", None), P("cells")),
        check_vma=False,
    )
```

time: 364 us -> 77.1 us (0.21)
  waiting for transfers between devices: 205 us -> 0 us
  starting transfers between devices: 89 us -> 0 us
  Pallas kernels: 0 us -> 73.2 us
  matrix products: 28.9 us -> 0 us
  blocking collectives: 16 us -> 0 us
  between operations: 14.9 us -> 0.64 us
  local copies, waits for them, and re-layouts: 8.86 us -> 3 us
    unnamed x2 -> x0, waiting for transfers between devices: 168 us -> none
    ppermute x12 -> x0, starting transfers between devices: 89 us -> none  [shifted(): return lax.ppermute(x, axis, [(i, (i + by) % size) for i in range(size)])]
    pallas_call x0 -> x1, Pallas kernels: none -> 73.2 us  [on_device(): pl.pallas_call(band_kernel, out_shape=(jax.ShapeDtypeStruct((blocks, SHIF...]
    ppermute x12 -> x0, waiting for transfers between devices: 37.1 us -> none  [shifted(): return lax.ppermute(x, axis, [(i, (i + by) % size) for i in range(size)])]
    dot_general x12 -> x0, matrix products: 28.9 us -> none  [the longest x5 15.2 us: panel_products(): jnp.einsum('fapij,fabpik->abjk', local_tiles, matched, preferred_element_...]
    psum x1 -> x0, blocking collectives: 16 us -> none  [on_device(): gradient = lax.psum(grad_part, 'freq')]
    another operation x1 -> x0, local copies, waits for them, and re-layouts: 5.68 us -> none  [on_device(): stacked = jnp.stack(blocks, axis=1)]
  transfers between devices with their start and end apart: 13 -> 0, of which waited for: 6 -> 0; matrix products, arithmetic and copies ran while one was open for 7% -> 0% of each run, Pallas kernels for 0% -> 0%
where the time goes in v3:
time: 77.1 us; the launch traced here: 76.9 us
  Pallas kernels  73.2 us (95%)
  local copies, waits for them, and re-layouts  3 us (4%)
    pallas_call x1, Pallas kernels, on_device(): pl.pallas_call(band_kernel, out_shape=(jax.ShapeDtypeStruct((blocks, SHIF...  73.2 us
    unnamed x2, local copies, waits for them, and re-layouts  3 us

profile of v3, /device:TPU:1, one launch (start us, length us, event | category | flops | bytes accessed | tf_op | source)
XLA Modules:
  0.0 76.9 jit_solution(6493526922750564002)
XLA Ops:
  0.6 73.2 %shard_map.59 = (f32[3,5,3,16,128]{4,3,2,1,0:T(8,128)}, f32[3,128]{1,0:T(4,128)}) custom-call(bf16[3,20,128,128]{3,2,1,0:T(8,128)(2,1)} %bitcast.2, s32[3,20]{1,0:T(4,128)} %tip_lists.1, s32[3]{0:T(128)} %counts.1, bf16[1,4096]{1,0:T(2,128)(2,1)} %resid_hbm.1), custom_call_target="tpu_custom_call" | custom-call | tf_op jit(solution)/shard_map/pallas_call | solution.py:520
  73.9 1.8 %copy.8 = f32[3,5,3,16,128]{4,3,2,1,0:T(8,128)} copy(f32[3,5,3,16,128]{4,3,2,1,0:T(8,128)} %get-tuple-element.8) | data formatting | bytes 737280
  75.6 1.2 %copy.9 = f32[384]{0:T(512)} copy(f32[384]{0:T(512)} %bitcast.3) | data formatting | bytes 3072

commit v4 on v3

--- a/solution.py
+++ b/solution.py
@@ -37,12 +37,12 @@
 
 def band_kernel(
     jac, tip_lists, counts, resid_hbm, band, grad,
-    raw, pk0, pk1, mate0, mate1, pan_d, pan_od, pan_u, pan_a, pan_oa,
+    raw, pk0, pk1, turned0, turned1, mate0, mate1, pan_d, pan_od, pan_u, pan_a, pan_oa, turned_a,
     resid, tab, tab_smem, far_tab, far_smem, mate_tab, mate_smem,
-    dense, left, odd_t, cross_t, prod, coded, y_in, y_sum, x_in, fin_out, fin_in,
+    dense, left, odd_t, cross_t, prod, coded, y_in, y_sum, fin_in, scale,
     g_own, g_in, g_sum, g_x,
     s_load, s_ts, s_tr, s_tl, s_ds, s_dr, s_us, s_ur, s_as, s_ar, s_ms, s_mr,
-    s_ods, s_odr, s_oas, s_oar, s_ys, s_yr, s_xls, s_xlr, s_fs, s_fr, s_gs, s_gr,
+    s_ods, s_odr, s_oas, s_oar, s_ys, s_yr, s_fs, s_fr, s_gs, s_gr,
 ):
     slots = jac.shape[1]
     half = slots // 2
@@ -62,7 +62,8 @@
     above = (f, lax.rem(d + 4, nd))
     x_pair = (f, d + 2 - 4 * hi)
     core_pair = (f, d + 1 - 2 * core)
-    xl_pair = (f + 1 - 2 * xl, d)
+    twin = f + 1 - 2 * xl
+    xl_pair = (twin, d)
 
     loads = []
     for b in range(NB):
@@ -72,7 +73,8 @@
         cp.start()
 
     barrier = pltpu.get_barrier_semaphore()
-    partners = [below, above, x_pair, core_pair] + [ydev(dy) for dy in range(1, NY)] + [xl_pair]
+    partners = [below, above, x_pair, core_pair] + [ydev(dy) for dy in range(1, NY)]
+    partners += [xl_pair, (twin, below[1]), (twin, above[1]), (twin, x_pair[1])]
     for dev in partners:
         pl.semaphore_signal(barrier, inc=1, device_id=dev, device_id_type=MESH)
 
@@ -96,7 +98,8 @@
     own_tab = pltpu.make_async_copy(tab, tab_smem, s_load.at[NB + 1])
     own_tab.start()
     zero = jnp.zeros((128, 128), jnp.bfloat16)
-    for panel in (pk0, pk1, mate0, mate1, pan_d, pan_od, pan_u, pan_a, pan_oa):
+    for panel in (pk0, pk1, turned0, turned1, mate0, mate1,
+                  pan_d, pan_od, pan_u, pan_a, pan_oa, turned_a):
         for block in panel:
             block[half] = zero
     for cp in loads:
@@ -105,11 +108,12 @@
 
     def pack(b):
         def step(i, carry):
-            pk0[b][i] = raw[b][tab_smem[1, b, i]]
-            pk1[b][i] = raw[b][tab_smem[1, 4 + b, i]]
+            even, odd = raw[b][tab_smem[1, b, i]], raw[b][tab_smem[1, 4 + b, i]]
+            pk0[b][i], pk1[b][i] = even, odd
+            turned0[b][i], turned1[b][i] = even.T, odd.T
             return carry
 
-        lax.fori_loop(0, half, step, 0)
+        lax.fori_loop(0, half, step, 0, unroll=2)
 
     pack(0)
     pl.semaphore_wait(barrier, len(partners))
@@ -127,7 +131,7 @@
             for b in range(NB)]
 
     d_copy = panel_copies(pk0, pan_d, s_ds, s_dr, below)
-    u_copy = panel_copies(pk1, pan_u, s_us, s_ur, above)
+    u_copy = panel_copies(turned1, pan_u, s_us, s_ur, above)
     a_copy0 = panel_copies(pk0, pan_a, s_as, s_ar, x_pair)
     a_copy1 = panel_copies(pk1, pan_a, s_as, s_ar, x_pair)
     m_copy = panel_copies(pk0, mate0, s_ms, s_mr, core_pair)
@@ -162,10 +166,10 @@
     def turn(panel, table, b, put_tile):
         def step(t, carry):
             at = pl.ds(pl.multiple_of(t * 128, 128), 128)
-            put_tile(at, panel[b][table(b, t)].T)
+            put_tile(at, panel[b][table(b, t)])
             return carry
 
-        lax.fori_loop(0, pairs, step, 0, unroll=2)
+        lax.fori_loop(0, pairs, step, 0, unroll=4)
 
     def fill(panel, table, b, which, lane):
         at = pl.ds(b * 256 + lane * 128, 128)
@@ -206,8 +210,8 @@
         left[0, below_rows, at] = jnp.broadcast_to(resid[:, pl.ds(t * 256, 128)], (16, 128))
         odd_t[below_rows, at] = jnp.broadcast_to(resid[:, pl.ds(t * 256 + 128, 128)], (16, 128))
     for b in range(NB):
-        turn(pk0, own_table(0), b, put_left(0, b))
-        turn(pk1, own_table(1), b, put_odd(b))
+        turn(turned0, own_table(0), b, put_left(0, b))
+        turn(turned1, own_table(1), b, put_odd(b))
         fill(pk0, own_table(0), b, 3, 0)
         fill(pk1, own_table(1), b, 1, 0)
 
@@ -238,44 +242,63 @@
         return remote(coded.at[take], y_in.at[dy - 1, pl.ds(coded_base(u) // NY, part)],
                       s_ys.at[i], s_yr.at[i], ydev(dy))
 
-    def xl_copy(u):
-        part = rows * COUNT[u]
-        give = pl.ds(pl.multiple_of(BASE[u] * 2 * rows + (1 - xl) * part, 8), part)
-        return remote(y_sum.at[give], x_in.at[pl.ds(BASE[u] * rows, part)],
-                      s_xls.at[u], s_xlr.at[u], xl_pair)
-
-    def fin_copy(u):
-        kind = UNITS[u][0]
+    def sums(u, half_of, first, n):
+        at = BASE[u] * 2 * rows + half_of * COUNT[u] * rows + first * rows
+        return pl.ds(pl.multiple_of(at, 8), n * rows)
+
+    def landed(u, first, n):
+        return pl.ds((BASE[u] + first) * rows, n * rows)
+
+    def owner_copies(u):
+        kind, n = UNITS[u][0], COUNT[u]
+
+        def copy(i, from_other, first, n, dev):
+            src = y_sum.at[sums(u, 1 - xl if from_other else xl, first, n)]
+            return remote(src, fin_in.at[from_other, landed(u, first, n)],
+                          s_fs.at[3 * u + i], s_fr.at[3 * u + i], dev)
+
+        if kind == "side":
+            owner = lax.rem(d - 4 * hi + nd, nd)
+            return [(None, copy(1, 1, 0, n, (twin, owner))), (1, copy(0, 0, 0, n, below))]
+        if kind == "cross":
+            return [(None, copy(1, 1, 0, n, (twin, x_pair[1]))), (None, copy(0, 0, 0, n, x_pair))]
         if kind == "z":
-            part = pl.ds((BASE[u] + NB) * rows, rows * NB)
-        else:
-            part = pl.ds(BASE[u] * rows, rows * COUNT[u])
-        dev = x_pair if kind == "cross" else below
-        return remote(fin_out.at[part], fin_in.at[part], s_fs.at[u], s_fr.at[u], dev)
+            return [(None, copy(2, 1, 0, NB, xl_pair)),
+                    (None, copy(1, 1, NB, NB, (twin, below[1]))), (None, copy(0, 0, NB, NB, below))]
+        return [(None, copy(1, 1, 0, n, xl_pair))]
+
+    def each(u, act):
+        for side_of, cp in owner_copies(u):
+            if side_of is None:
+                act(cp)
+            else:
+                pl.when(hi == side_of)(lambda: act(cp))
+
+    line = lax.broadcasted_iota(jnp.int32, (SCALE_ROWS, 128), 0)
 
     def send(u):
         n = COUNT[u]
 
         def body():
-            def peak(i, top):
-                at = pl.ds(pl.multiple_of(BASE[u] * 128 + i * 128, 128), 128)
-                return jnp.maximum(top, jnp.abs(prod[at]))
-
-            top = lax.fori_loop(0, n, peak, jnp.zeros((128, 128), jnp.float32))
-            top = jnp.full((16, 128), jnp.max(top), jnp.float32)
-            power = jnp.ceil(jnp.log2(jnp.maximum(top, 1e-33)) + 1e-3)
-            up = jnp.exp2(15.0 - power)[:1] * (32766.0 / 32768.0)
-            for part in range(NY):
-                start = coded_base(u) + part * y_part(u)
-
-                def code(i, carry):
-                    src = pl.ds(pl.multiple_of(BASE[u] * 128 + part * n * 32 + i * 32, 32), 32)
-                    dst = pl.ds(pl.multiple_of(start + i * 32, 16), 32)
-                    coded[dst] = jnp.round(prod[src] * up).astype(jnp.int32).astype(jnp.int16)
-                    return carry
-
-                lax.fori_loop(0, n, code, 0)
-                coded[pl.ds(start + n * 32, SCALE_ROWS)] = power.astype(jnp.int32).astype(jnp.int16)
+            parts = [lax.rem(y + dy, NY) for dy in range(1, NY)]
+
+            def code(i, powers):
+                new = []
+                for part, known in zip(parts, powers):
+                    src = pl.multiple_of(BASE[u] * 128 + part * n * 32 + i * 32, 32)
+                    dst = pl.multiple_of(coded_base(u) + part * y_part(u) + i * 32, 16)
+                    value = prod[pl.ds(src, 32)]
+                    top = jnp.maximum(jnp.max(jnp.abs(value), axis=0, keepdims=True), 1e-33)
+                    power = jnp.ceil(jnp.log2(top) + 1e-3)
+                    up = jnp.exp2(15.0 - power) * (32766.0 / 32768.0)
+                    coded[pl.ds(dst, 32)] = jnp.round(value * up).astype(jnp.int32).astype(jnp.int16)
+                    new.append(jnp.where(line == i, power, known))
+                return tuple(new)
+
+            powers = lax.fori_loop(0, n, code, (jnp.zeros((SCALE_ROWS, 128), jnp.float32),) * (NY - 1))
+            for part, power in zip(parts, powers):
+                dst = pl.multiple_of(coded_base(u) + part * y_part(u) + n * 32, 16)
+                coded[pl.ds(dst, SCALE_ROWS)] = power.astype(jnp.int32).astype(jnp.int16)
             for dy in range(1, NY):
                 y_copy(u, dy).start()
 
@@ -285,12 +308,11 @@
         n = COUNT[u]
 
         def body():
-            down = []
             for dy in range(1, NY):
                 y_copy(u, dy).wait_recv()
                 power = y_in[dy - 1, pl.ds(coded_base(u) // NY + n * 32, SCALE_ROWS)]
                 power = power.astype(jnp.int32).astype(jnp.float32)
-                down.append(jnp.exp2(power - 15.0)[:1] * (32768.0 / 32766.0))
+                scale[dy - 1] = jnp.exp2(power - 15.0) * (32768.0 / 32766.0)
 
             def step(i, carry):
                 at = pl.ds(pl.multiple_of(BASE[u] * 128 + y * n * 32 + i * 32, 32), 32)
@@ -298,74 +320,49 @@
                 for dy in range(1, NY):
                     src = pl.ds(pl.multiple_of(coded_base(u) // NY + i * 32, 16), 32)
                     part = y_in[dy - 1, src].astype(jnp.int32).astype(jnp.float32)
-                    total = total + part * down[dy - 1]
+                    total = total + part * scale[dy - 1, pl.ds(i, 1)]
                 y_sum[pl.ds(pl.multiple_of(BASE[u] * 32 + i * 32, 32), 32)] = total
                 return carry
 
             lax.fori_loop(0, n, step, 0)
-            xl_copy(u).start()
+            each(u, lambda cp: cp.start())
 
         on(u, body)
 
-    def block_rows(u, i):
-        return pl.ds((BASE[u] + i) * rows, rows)
-
-    def x_finish(u):
-        kind, _, _, blocks = UNITS[u]
-        part = rows * COUNT[u]
-
-        def body():
-            xl_copy(u).wait_recv()
-            keep = pl.ds(pl.multiple_of(BASE[u] * 2 * rows + xl * part, 8), part)
-            fin_out[pl.ds(BASE[u] * rows, part)] = y_sum[keep] + x_in[pl.ds(BASE[u] * rows, part)]
-            if kind == "side":
-                pl.when(hi == 1)(lambda: fin_copy(u).start())
-            elif kind in ("cross", "z"):
-                fin_copy(u).start()
-
-        on(u, body)
+    def here(u, i):
+        return y_sum[sums(u, xl, i, 1)] + fin_in[1, landed(u, i, 1)]
+
+    def arrived(u, i):
+        return fin_in[0, landed(u, i, 1)] + fin_in[1, landed(u, i, 1)]
 
     def fin_finish(u):
         kind, _, _, blocks = UNITS[u]
 
         def body():
+            each(u, lambda cp: cp.wait_recv())
             if kind in ("own", "mate"):
                 for i, (a, lane, b) in enumerate(blocks):
-                    band[a, lane, b] = fin_out[block_rows(u, i)]
-            elif kind == "z":
-                for i, (a, lane, b) in enumerate(blocks[:NB]):
-                    z_own[(a, lane, b)] = (u, i)
-                fin_copy(u).wait_recv()
+                    band[a, lane, b] = here(u, i)
             elif kind == "side":
-                def from_here():
-                    for i, (a, lane, b) in enumerate(blocks):
-                        band[a, 3 - 2 * core if lane else 2, b] = fin_out[block_rows(u, i)]
-
-                def from_above():
-                    fin_copy(u).wait_recv()
-                    for i, (a, lane, b) in enumerate(blocks):
-                        band[a, 3 - 2 * core if lane else 2, b] = fin_in[block_rows(u, i)]
-
-                pl.when(hi == 0)(from_here)
-                pl.when(hi == 1)(from_above)
-            else:
-                fin_copy(u).wait_recv()
+                for side_of, value in ((0, here), (1, arrived)):
+                    @pl.when(hi == side_of)
+                    def _():
+                        for i, (a, lane, b) in enumerate(blocks):
+                            band[a, 3 - 2 * core if lane else 2, b] = value(u, i)
+            elif kind == "cross":
                 for i, (a, lane, b) in enumerate(blocks):
                     k = 3 - 2 * core if lane else 2
-                    band[a, k, b] = band[a, k, b] + fin_in[block_rows(u, i)]
+                    band[a, k, b] = band[a, k, b] + arrived(u, i)
 
         on(u, body)
 
-    z_own = {}
+    z_down = {block: (u, i) for u in range(len(UNITS)) if UNITS[u][0] == "z"
+              for i, block in enumerate(UNITS[u][3][:NB])}
 
     def z_place(u):
-        _, _, _, blocks = UNITS[u]
-
         def body():
-            for i, (a, lane, b) in enumerate(blocks[NB:]):
-                v, j = z_own[(a, lane, b)]
-                k = 3 if lane else 4
-                band[a, k, b] = fin_out[block_rows(v, j)] + fin_in[block_rows(u, NB + i)]
+            for i, (a, lane, b) in enumerate(UNITS[u][3][NB:]):
+                band[a, 3 if lane else 4, b] = here(*z_down[(a, lane, b)]) + arrived(u, NB + i)
 
         on(u, body)
 
@@ -425,7 +422,13 @@
 
         fill(pan_d, far_table(1, 0), s, 0, 0)
         fill(pan_a, lambda b, t: far_smem[3, hi * 4 + b, t], s, 2, 0)
-        turn(pan_a, lambda b, t: far_smem[3, hi * 4 + b, t], s, put_cross(s))
+
+        def turn_tile(i, carry):
+            turned_a[s][i] = pan_a[s][i].T
+            return carry
+
+        lax.fori_loop(0, half, turn_tile, 0, unroll=2)
+        turn(turned_a, lambda b, t: far_smem[3, hi * 4 + b, t], s, put_cross(s))
         u_copy[s].wait_recv()
         turn(pan_u, far_table(2, 1), s, put_left(1, s))
         od_copy[s].wait_recv()
@@ -461,25 +464,15 @@
             y_finish(u)
         if s > 0:
             for u in step_units(s - 2):
-                x_finish(u)
-        if s > 1:
-            for u in step_units(s - 3):
                 fin_finish(u)
 
     gx_copy.wait_recv()
     for b in range(NB):
         at = pl.ds(b * 128, 128)
         grad[pl.ds(b, 1), :] = g_sum[pl.ds(0, 1), at] + g_x[pl.ds(0, 1), at]
-    last = step_units(NB - 1)
-    for u in step_units(NB - 2):
-        x_finish(u)
-    for u in last:
+    for u in step_units(NB - 1):
         y_finish(u)
-    for u in step_units(NB - 3):
-        fin_finish(u)
-    for u in last:
-        x_finish(u)
-    for u in step_units(NB - 2) + last:
+    for u in step_units(NB - 2) + step_units(NB - 1):
         fin_finish(u)
     for u in range(len(UNITS)):
         if UNITS[u][0] == "z":
@@ -488,16 +481,10 @@
     for cp in t_copy + [mt_copy] + d_copy + u_copy + a_copy0 + m_copy + od_copy + oa_copy:
         cp.wait_send()
     for u in range(len(UNITS)):
-        kind = UNITS[u][0]
-
         def drain():
             for dy in range(1, NY):
                 y_copy(u, dy).wait_send()
-            xl_copy(u).wait_send()
-            if kind == "side":
-                pl.when(hi == 1)(lambda: fin_copy(u).wait_send())
-            elif kind in ("cross", "z"):
-                fin_copy(u).wait_send()
+            each(u, lambda cp: cp.wait_send())
 
         on(u, drain)
     for dy in range(1, NY):
@@ -531,20 +518,20 @@
         ],
         out_specs=(pl.BlockSpec(memory_space=pltpu.VMEM), pl.BlockSpec(memory_space=pltpu.VMEM)),
         scratch_shapes=[
-            [vm((slots, tile, tile), bf16)] * blocks, half, half, half, half, half, half, half, half, half,
+            [vm((slots, tile, tile), bf16)] * blocks, *[half] * 12,
             vm((1, depth), bf16), vm((2, 8, 128), i32), pltpu.SMEM((2, 8, 128), i32),
             vm((4, 8, 128), i32), pltpu.SMEM((4, 8, 128), i32),
             vm((3, 8, 128), i32), pltpu.SMEM((3, 8, 128), i32),
             vm((4, depth // 2, 2 * width), bf16), vm((2, width + 16, depth // 2), bf16),
             vm((width + 16, depth // 2), bf16), vm((width, depth // 2), bf16),
             vm((TOTAL * tile, tile), f32), vm((coded, tile), i16), vm((NY - 1, coded // NY, tile), i16),
-            vm((TOTAL * 2 * rows, tile), f32), vm((TOTAL * rows, tile), f32),
-            vm((TOTAL * rows, tile), f32), vm((TOTAL * rows, tile), f32),
+            vm((TOTAL * 2 * rows, tile), f32), vm((2, TOTAL * rows, tile), f32),
+            vm((NY - 1, SCALE_ROWS, tile), f32),
             vm((8, width), f32), vm((NY, 8, width), f32), vm((8, width), f32), vm((8, width), f32),
             dma((blocks + 2,)), dma((5,)), dma((5,)), dma((2,)),
             *per_block, *per_block, *per_block, dma((2 * blocks,)), dma((2 * blocks,)),
             *per_block, *per_block,
-            dma((n * (NY - 1),)), dma((n * (NY - 1),)), dma((n,)), dma((n,)), dma((n,)), dma((n,)),
+            dma((n * (NY - 1),)), dma((n * (NY - 1),)), dma((3 * n,)), dma((3 * n,)),
             dma((NY,)), dma((NY,)),
         ],
         compiler_params=pltpu.CompilerParams(

time: 77.1 us -> 74 us (0.960)
  Pallas kernels: 73.2 us -> 70.1 us
    pallas_call x1, Pallas kernels: 73.2 us -> 70.1 us  [on_device(): pl.pallas_call(band_kernel, out_shape=(jax.ShapeDtypeStruct((blocks, SHIF...]
where the time goes in v4:
time: 74 us; the launch traced here: 73.8 us
  Pallas kernels  70.1 us (95%)
  local copies, waits for them, and re-layouts  3 us (4%)
    pallas_call x1, Pallas kernels, on_device(): pl.pallas_call(band_kernel, out_shape=(jax.ShapeDtypeStruct((blocks, SHIF...  70.1 us
    unnamed x2, local copies, waits for them, and re-layouts  3 us

profile of v4, /device:TPU:1, one launch (start us, length us, event | category | flops | bytes accessed | tf_op | source)
XLA Modules:
  0.0 73.8 jit_solution(11547992348870949570)
XLA Ops:
  0.6 70.1 %shard_map.59 = (f32[3,5,3,16,128]{4,3,2,1,0:T(8,128)}, f32[3,128]{1,0:T(4,128)}) custom-call(bf16[3,20,128,128]{3,2,1,0:T(8,128)(2,1)} %bitcast.2, s32[3,20]{1,0:T(4,128)} %tip_lists.1, s32[3]{0:T(128)} %counts.1, bf16[1,4096]{1,0:T(2,128)(2,1)} %resid_hbm.1), custom_call_target="tpu_custom_call" | custom-call | tf_op jit(solution)/shard_map/pallas_call | solution.py:507
  70.8 1.8 %copy.8 = f32[3,5,3,16,128]{4,3,2,1,0:T(8,128)} copy(f32[3,5,3,16,128]{4,3,2,1,0:T(8,128)} %get-tuple-element.8) | data formatting | bytes 737280
  72.5 1.2 %copy.9 = f32[384]{0:T(512)} copy(f32[384]{0:T(512)} %bitcast.3) | data formatting | bytes 3072

commit v5 on v4

--- a/solution.py
+++ b/solution.py
@@ -39,7 +39,7 @@
     jac, tip_lists, counts, resid_hbm, band, grad,
     raw, pk0, pk1, turned0, turned1, mate0, mate1, pan_d, pan_od, pan_u, pan_a, pan_oa, turned_a,
     resid, tab, tab_smem, far_tab, far_smem, mate_tab, mate_smem,
-    dense, left, odd_t, cross_t, prod, coded, y_in, y_sum, fin_in, scale,
+    dense, alone, left, odd_t, cross_t, prod, coded, y_in, y_sum, fin_in, scale,
     g_own, g_in, g_sum, g_x,
     s_load, s_ts, s_tr, s_tl, s_ds, s_dr, s_us, s_ur, s_as, s_ar, s_ms, s_mr,
     s_ods, s_odr, s_oas, s_oar, s_ys, s_yr, s_fs, s_fr, s_gs, s_gr,
@@ -180,6 +180,15 @@
 
         lax.fori_loop(0, pairs, step, 0, unroll=4)
 
+    def fill_alone(panel, table, b, parity):
+        at = pl.ds(b * 128, 128)
+
+        def step(t, carry):
+            alone[parity, pl.ds(pl.multiple_of(t * 128, 128), 128), at] = panel[b][table(b, t)]
+            return carry
+
+        lax.fori_loop(0, pairs, step, 0, unroll=4)
+
     def own_table(parity):
         return lambda b, t: tab_smem[0, parity * 4 + b, t]
 
@@ -212,15 +221,8 @@
     for b in range(NB):
         turn(turned0, own_table(0), b, put_left(0, b))
         turn(turned1, own_table(1), b, put_odd(b))
-        fill(pk0, own_table(0), b, 3, 0)
-        fill(pk1, own_table(1), b, 1, 0)
-
-    for cp in t_copy:
-        cp.wait_recv()
-    mt_copy.start()
-    far_load = pltpu.make_async_copy(far_tab, far_smem, s_tl.at[0])
-    far_load.start()
-    far_load.wait()
+        fill_alone(pk0, own_table(0), b, 0)
+        fill_alone(pk1, own_table(1), b, 1)
 
     def on(u, body):
         which = UNITS[u][1]
@@ -380,19 +382,12 @@
     def dot(a, b):
         return jnp.dot(a, b, preferred_element_type=jnp.float32)
 
-    for b in range(NB):
-        m_copy[b].wait_recv()
-        m_copy[NB + b].wait_recv()
-        fill(mate0, far_table(0, 0), b, 3, 1)
-        fill(mate1, far_table(0, 1), b, 1, 1)
-        at = pl.ds(b * 256, 256)
-        out = dot(left[0], dense[3, :, at]) + dot(odd_t[...], dense[1, :, at])
+    out = dot(left[0], alone[0]) + dot(odd_t[...], alone[1])
+    for b in range(NB):
         for a in range(NB):
-            put(0, b * NB + a, out[a * 128:(a + 1) * 128, :128])
-            put(1, b * NB + a, out[a * 128:(a + 1) * 128, 128:])
-        g_own[:, pl.ds(b * 128, 128)] = out[NB * 128:NB * 128 + 8, :128]
+            put(0, b * NB + a, out[a * 128:(a + 1) * 128, b * 128:(b + 1) * 128])
+    g_own[...] = out[NB * 128:NB * 128 + 8]
     send(0)
-    send(1)
 
     def g_copy(dy):
         return remote(g_own, g_in.at[y], s_gs.at[dy - 1], s_gr.at[dy - 1], ydev(dy))
@@ -405,6 +400,30 @@
         g_copy(dy).start()
     g_in[y] = g_own[...]
 
+    for cp in t_copy:
+        cp.wait_recv()
+    mt_copy.start()
+    far_load = pltpu.make_async_copy(far_tab, far_smem, s_tl.at[0])
+    far_load.start()
+    far_load.wait()
+    for cp in m_copy:
+        cp.wait_recv()
+
+    @pl.when(core == 0)
+    def _():
+        for b in range(NB):
+            fill_alone(mate0, far_table(0, 0), b, 0)
+            fill_alone(mate1, far_table(0, 1), b, 1)
+        rows_of = pl.ds(0, NB * 128)
+        out = dot(left[0, rows_of], alone[0]) + dot(odd_t[rows_of], alone[1])
+        for b in range(NB):
+            for a in range(NB):
+                put(1, b * NB + a, out[a * 128:(a + 1) * 128, b * 128:(b + 1) * 128])
+
+    send(1)
+    for b in range(NB):
+        fill(pk1, own_table(1), b, 1, 0)
+        fill(mate1, far_table(0, 1), b, 1, 1)
     mt_copy.wait_recv()
     mate_load = pltpu.make_async_copy(mate_tab, mate_smem, s_tl.at[1])
     mate_load.start()
@@ -470,9 +489,11 @@
     for b in range(NB):
         at = pl.ds(b * 128, 128)
         grad[pl.ds(b, 1), :] = g_sum[pl.ds(0, 1), at] + g_x[pl.ds(0, 1), at]
+    for u in step_units(NB - 2):
+        fin_finish(u)
     for u in step_units(NB - 1):
         y_finish(u)
-    for u in step_units(NB - 2) + step_units(NB - 1):
+    for u in step_units(NB - 1):
         fin_finish(u)
     for u in range(len(UNITS)):
         if UNITS[u][0] == "z":
@@ -522,7 +543,8 @@
             vm((1, depth), bf16), vm((2, 8, 128), i32), pltpu.SMEM((2, 8, 128), i32),
             vm((4, 8, 128), i32), pltpu.SMEM((4, 8, 128), i32),
             vm((3, 8, 128), i32), pltpu.SMEM((3, 8, 128), i32),
-            vm((4, depth // 2, 2 * width), bf16), vm((2, width + 16, depth // 2), bf16),
+            vm((3, depth // 2, 2 * width), bf16), vm((2, depth // 2, width), bf16),
+            vm((2, width + 16, depth // 2), bf16),
             vm((width + 16, depth // 2), bf16), vm((width, depth // 2), bf16),
             vm((TOTAL * tile, tile), f32), vm((coded, tile), i16), vm((NY - 1, coded // NY, tile), i16),
             vm((TOTAL * 2 * rows, tile), f32), vm((2, TOTAL * rows, tile), f32),

time: 74 us -> 69.9 us (0.945)
  Pallas kernels: 70.1 us -> 66.1 us
    pallas_call x1, Pallas kernels: 70.1 us -> 66.1 us  [on_device(): pl.pallas_call(band_kernel, out_shape=(jax.ShapeDtypeStruct((blocks, SHIF...]
where the time goes in v5:
time: 69.9 us; the launch traced here: 69.7 us
  Pallas kernels  66.1 us (95%)
  local copies, waits for them, and re-layouts  3 us (4%)
    pallas_call x1, Pallas kernels, on_device(): pl.pallas_call(band_kernel, out_shape=(jax.ShapeDtypeStruct((blocks, SHIF...  66.1 us
    unnamed x2, local copies, waits for them, and re-layouts  3 us

profile of v5, /device:TPU:1, one launch (start us, length us, event | category | flops | bytes accessed | tf_op | source)
XLA Modules:
  0.0 69.7 jit_solution(2078608091483337210)
XLA Ops:
  0.6 66.1 %shard_map.59 = (f32[3,5,3,16,128]{4,3,2,1,0:T(8,128)}, f32[3,128]{1,0:T(4,128)}) custom-call(bf16[3,20,128,128]{3,2,1,0:T(8,128)(2,1)} %bitcast.2, s32[3,20]{1,0:T(4,128)} %tip_lists.1, s32[3]{0:T(128)} %counts.1, bf16[1,4096]{1,0:T(2,128)(2,1)} %resid_hbm.1), custom_call_target="tpu_custom_call" | custom-call | tf_op jit(solution)/shard_map/pallas_call | solution.py:528
  66.7 1.8 %copy.8 = f32[3,5,3,16,128]{4,3,2,1,0:T(8,128)} copy(f32[3,5,3,16,128]{4,3,2,1,0:T(8,128)} %get-tuple-element.8) | data formatting | bytes 737280
  68.4 1.2 %copy.9 = f32[384]{0:T(512)} copy(f32[384]{0:T(512)} %bitcast.3) | data formatting | bytes 3072

commit v6 on v5

--- a/solution.py
+++ b/solution.py
@@ -20,8 +20,8 @@
     for s in range(NB):
         grid = [(a, lane, s) for a in range(s + 1) for lane in range(2)]
         grid += [(s, lane, b) for b in range(s) for lane in range(2)]
-        units.append(("side", None, s, grid))
-        units.append(("cross", None, s, grid))
+        units.append(("grid", None, s, grid))
+        units.append(("line", None, s, [(i, lane) for i in range(NB) for lane in range(2)]))
         for lane in range(2):
             down = [(a, lane, s) for a in range(NB)]
             up = [(s, lane, b) for b in range(NB)]
@@ -39,7 +39,7 @@
     jac, tip_lists, counts, resid_hbm, band, grad,
     raw, pk0, pk1, turned0, turned1, mate0, mate1, pan_d, pan_od, pan_u, pan_a, pan_oa, turned_a,
     resid, tab, tab_smem, far_tab, far_smem, mate_tab, mate_smem,
-    dense, alone, left, odd_t, cross_t, prod, coded, y_in, y_sum, fin_in, scale,
+    dense, alone, left, odd_t, prod, coded, y_in, y_sum, fin_in, scale,
     g_own, g_in, g_sum, g_x,
     s_load, s_ts, s_tr, s_tl, s_ds, s_dr, s_us, s_ur, s_as, s_ar, s_ms, s_mr,
     s_ods, s_odr, s_oas, s_oar, s_ys, s_yr, s_fs, s_fr, s_gs, s_gr,
@@ -208,11 +208,6 @@
             odd_t[pl.ds(b * 128, 128), at] = tile
         return put
 
-    def put_cross(b):
-        def put(at, tile):
-            cross_t[pl.ds(b * 128, 128), at] = tile
-        return put
-
     below_rows = pl.ds(NB * 128, 16)
     for t in range(pairs):
         at = pl.ds(t * 128, 128)
@@ -256,21 +251,24 @@
 
         def copy(i, from_other, first, n, dev):
             src = y_sum.at[sums(u, 1 - xl if from_other else xl, first, n)]
-            return remote(src, fin_in.at[from_other, landed(u, first, n)],
-                          s_fs.at[3 * u + i], s_fr.at[3 * u + i], dev)
-
-        if kind == "side":
-            owner = lax.rem(d - 4 * hi + nd, nd)
-            return [(None, copy(1, 1, 0, n, (twin, owner))), (1, copy(0, 0, 0, n, below))]
-        if kind == "cross":
-            return [(None, copy(1, 1, 0, n, (twin, x_pair[1]))), (None, copy(0, 0, 0, n, x_pair))]
+            return remote(src, fin_in.at[i, landed(u, first, n)],
+                          s_fs.at[5 * u + i], s_fr.at[5 * u + i], dev)
+
+        if kind == "line":
+            return [(0, 0, copy(2, 1, 0, n, xl_pair)),
+                    (1, 0, copy(1, 1, 0, n, (twin, x_pair[1]))), (1, 0, copy(0, 0, 0, n, x_pair))]
+        if kind == "grid":
+            return [(0, 1, copy(1, 1, 0, n, (twin, x_pair[1]))), (0, 1, copy(0, 0, 0, n, x_pair)),
+                    (1, 1, copy(4, 1, 0, n, (twin, below[1]))), (1, 1, copy(3, 0, 0, n, below))]
         if kind == "z":
-            return [(None, copy(2, 1, 0, NB, xl_pair)),
-                    (None, copy(1, 1, NB, NB, (twin, below[1]))), (None, copy(0, 0, NB, NB, below))]
-        return [(None, copy(1, 1, 0, n, xl_pair))]
-
-    def each(u, act):
-        for side_of, cp in owner_copies(u):
+            return [(None, None, copy(2, 1, 0, NB, xl_pair)),
+                    (None, None, copy(1, 1, NB, NB, (twin, below[1]))),
+                    (None, None, copy(0, 0, NB, NB, below))]
+        return [(None, None, copy(2, 1, 0, n, xl_pair))]
+
+    def each(u, receives, act):
+        for sends_at, receives_at, cp in owner_copies(u):
+            side_of = receives_at if receives else sends_at
             if side_of is None:
                 act(cp)
             else:
@@ -327,46 +325,57 @@
                 return carry
 
             lax.fori_loop(0, n, step, 0)
-            each(u, lambda cp: cp.start())
+            each(u, False, lambda cp: cp.start())
 
         on(u, body)
 
     def here(u, i):
-        return y_sum[sums(u, xl, i, 1)] + fin_in[1, landed(u, i, 1)]
-
-    def arrived(u, i):
-        return fin_in[0, landed(u, i, 1)] + fin_in[1, landed(u, i, 1)]
-
-    def fin_finish(u):
-        kind, _, _, blocks = UNITS[u]
-
-        def body():
-            each(u, lambda cp: cp.wait_recv())
-            if kind in ("own", "mate"):
-                for i, (a, lane, b) in enumerate(blocks):
-                    band[a, lane, b] = here(u, i)
-            elif kind == "side":
-                for side_of, value in ((0, here), (1, arrived)):
-                    @pl.when(hi == side_of)
-                    def _():
-                        for i, (a, lane, b) in enumerate(blocks):
-                            band[a, 3 - 2 * core if lane else 2, b] = value(u, i)
-            elif kind == "cross":
-                for i, (a, lane, b) in enumerate(blocks):
-                    k = 3 - 2 * core if lane else 2
-                    band[a, k, b] = band[a, k, b] + arrived(u, i)
-
-        on(u, body)
-
-    z_down = {block: (u, i) for u in range(len(UNITS)) if UNITS[u][0] == "z"
-              for i, block in enumerate(UNITS[u][3][:NB])}
-
-    def z_place(u):
-        def body():
-            for i, (a, lane, b) in enumerate(UNITS[u][3][NB:]):
-                band[a, 3 if lane else 4, b] = here(*z_down[(a, lane, b)]) + arrived(u, NB + i)
-
-        on(u, body)
+        return y_sum[sums(u, xl, i, 1)] + fin_in[2, landed(u, i, 1)]
+
+    def arrived(u, i, first=0):
+        return fin_in[first, landed(u, i, 1)] + fin_in[first + 1, landed(u, i, 1)]
+
+    def unit_of(kind, s, which=None):
+        return next(u for u in range(len(UNITS))
+                    if UNITS[u][0] == kind and UNITS[u][1] == which and UNITS[u][2] == s)
+
+    def fin_finish(s):
+        for u in step_units(s):
+            on(u, lambda: each(u, True, lambda cp: cp.wait_recv()))
+        if s < 0:
+            for u in step_units(s):
+                def copy_out():
+                    for i, (a, lane, b) in enumerate(UNITS[u][3]):
+                        band[a, lane, b] = here(u, i)
+                on(u, copy_out)
+            return
+        done = [(a, b) for a in range(NB) for b in range(NB) if max(a, b) == s]
+
+        def k_of(lane):
+            return 3 - 2 * core if lane else 2
+
+        @pl.when(hi == 0)
+        def _():
+            for a, b in done:
+                for lane in range(2):
+                    band[a, k_of(lane), b] = (here(unit_of("line", b), 2 * a + lane)
+                                              + arrived(unit_of("line", a), 2 * b + lane))
+
+        @pl.when(hi == 1)
+        def _():
+            u = unit_of("grid", s)
+            for i, (a, lane, b) in enumerate(UNITS[u][3]):
+                band[a, k_of(lane), b] = arrived(u, i) + arrived(u, i, 3)
+
+        for lane, which in enumerate((None, 1)):
+            def z_blocks():
+                for a, b in done:
+                    band[a, 3 if lane else 4, b] = (here(unit_of("z", b, which), a)
+                                                    + arrived(unit_of("z", a, which), NB + b))
+            on(unit_of("z", s, which), z_blocks)
+
+    def step_units(s):
+        return [u for u in range(len(UNITS)) if UNITS[u][2] == s]
 
     def put(u, i, block):
         for g in range(2 * NY):
@@ -429,11 +438,8 @@
     mate_load.start()
     mate_load.wait()
 
-    def step_units(s):
-        return [u for u in range(len(UNITS)) if UNITS[u][2] == s]
-
     for s in range(NB):
-        side, cross, z_self, z_mate = step_units(s)
+        grid, line_of, z_self, z_mate = step_units(s)
         d_copy[s].wait_recv()
         od_copy[s].start()
         a_copy0[s].wait_recv()
@@ -447,7 +453,7 @@
             return carry
 
         lax.fori_loop(0, half, turn_tile, 0, unroll=2)
-        turn(turned_a, lambda b, t: far_smem[3, hi * 4 + b, t], s, put_cross(s))
+        turn(turned_a, lambda b, t: far_smem[3, hi * 4 + b, t], s, put_left(2, s))
         u_copy[s].wait_recv()
         turn(pan_u, far_table(2, 1), s, put_left(1, s))
         od_copy[s].wait_recv()
@@ -456,16 +462,25 @@
         fill(pan_oa, lambda b, t: mate_smem[2, hi * 4 + b, t], s, 2, 1)
 
         upto, now = list(range(s + 1)), pl.ds(s * 256, 256)
-        put_grid(cross, dot(cross_t[pl.ds(0, 128 * (s + 1)), :], dense[hi, :, now]), upto, [s])
+        put_grid(grid, dot(left[2 - hi, pl.ds(0, 128 * (s + 1)), :], dense[2 * hi, :, now]), upto, [s])
         if s > 0:
-            put_grid(cross, dot(cross_t[pl.ds(128 * s, 128), :], dense[hi, :, pl.ds(0, 256 * s)]),
+            put_grid(grid, dot(left[2 - hi, pl.ds(128 * s, 128), :], dense[2 * hi, :, pl.ds(0, 256 * s)]),
                      [s], list(range(s)))
-        send(cross)
-        put_grid(side, dot(left[hi, pl.ds(0, 128 * (s + 1)), :], dense[2, :, now]), upto, [s])
-        if s > 0:
-            put_grid(side, dot(left[hi, pl.ds(128 * s, 128), :], dense[2, :, pl.ds(0, 256 * s)]),
-                     [s], list(range(s)))
-        send(side)
+        send(grid)
+
+        @pl.when(hi == 0)
+        def _():
+            out = dot(left[0, pl.ds(0, NB * 128), :], dense[2, :, now])
+            for i, (a, lane) in enumerate(UNITS[line_of][3]):
+                put(line_of, i, out[a * 128:(a + 1) * 128, lane * 128:(lane + 1) * 128])
+
+        @pl.when(hi == 1)
+        def _():
+            out = dot(left[2, pl.ds(128 * s, 128), :], dense[1])
+            for i, (b, lane) in enumerate(UNITS[line_of][3]):
+                put(line_of, i, out[:, b * 256 + lane * 128:b * 256 + (lane + 1) * 128])
+
+        send(line_of)
         down = dot(left[0, pl.ds(0, NB * 128), :], dense[0, :, now])
         up = dot(left[1, pl.ds(128 * s, 128), :], dense[1])
         for i in range(NB):
@@ -482,22 +497,16 @@
         for u in step_units(s - 1):
             y_finish(u)
         if s > 0:
-            for u in step_units(s - 2):
-                fin_finish(u)
+            fin_finish(s - 2)
 
     gx_copy.wait_recv()
     for b in range(NB):
         at = pl.ds(b * 128, 128)
         grad[pl.ds(b, 1), :] = g_sum[pl.ds(0, 1), at] + g_x[pl.ds(0, 1), at]
-    for u in step_units(NB - 2):
-        fin_finish(u)
+    fin_finish(NB - 2)
     for u in step_units(NB - 1):
         y_finish(u)
-    for u in step_units(NB - 1):
-        fin_finish(u)
-    for u in range(len(UNITS)):
-        if UNITS[u][0] == "z":
-            z_place(u)
+    fin_finish(NB - 1)
 
     for cp in t_copy + [mt_copy] + d_copy + u_copy + a_copy0 + m_copy + od_copy + oa_copy:
         cp.wait_send()
@@ -505,7 +514,7 @@
         def drain():
             for dy in range(1, NY):
                 y_copy(u, dy).wait_send()
-            each(u, lambda cp: cp.wait_send())
+            each(u, False, lambda cp: cp.wait_send())
 
         on(u, drain)
     for dy in range(1, NY):
@@ -544,16 +553,15 @@
             vm((4, 8, 128), i32), pltpu.SMEM((4, 8, 128), i32),
             vm((3, 8, 128), i32), pltpu.SMEM((3, 8, 128), i32),
             vm((3, depth // 2, 2 * width), bf16), vm((2, depth // 2, width), bf16),
-            vm((2, width + 16, depth // 2), bf16),
-            vm((width + 16, depth // 2), bf16), vm((width, depth // 2), bf16),
+            vm((3, width + 16, depth // 2), bf16), vm((width + 16, depth // 2), bf16),
             vm((TOTAL * tile, tile), f32), vm((coded, tile), i16), vm((NY - 1, coded // NY, tile), i16),
-            vm((TOTAL * 2 * rows, tile), f32), vm((2, TOTAL * rows, tile), f32),
+            vm((TOTAL * 2 * rows, tile), f32), vm((5, TOTAL * rows, tile), f32),
             vm((NY - 1, SCALE_ROWS, tile), f32),
             vm((8, width), f32), vm((NY, 8, width), f32), vm((8, width), f32), vm((8, width), f32),
             dma((blocks + 2,)), dma((5,)), dma((5,)), dma((2,)),
             *per_block, *per_block, *per_block, dma((2 * blocks,)), dma((2 * blocks,)),
             *per_block, *per_block,
-            dma((n * (NY - 1),)), dma((n * (NY - 1),)), dma((3 * n,)), dma((3 * n,)),
+            dma((n * (NY - 1),)), dma((n * (NY - 1),)), dma((5 * n,)), dma((5 * n,)),
             dma((NY,)), dma((NY,)),
         ],
         compiler_params=pltpu.CompilerParams(

time: 69.9 us -> 68.5 us (0.980)
  Pallas kernels: 66.1 us -> 64.6 us
    pallas_call x1, Pallas kernels: 66.1 us -> 64.6 us  [on_device(): pl.pallas_call(band_kernel, out_shape=(jax.ShapeDtypeStruct((blocks, SHIF...]
where the time goes in v6:
time: 68.5 us; the launch traced here: 68.2 us
  Pallas kernels  64.6 us (94%)
  local copies, waits for them, and re-layouts  3 us (4%)
    pallas_call x1, Pallas kernels, on_device(): pl.pallas_call(band_kernel, out_shape=(jax.ShapeDtypeStruct((blocks, SHIF...  64.6 us
    unnamed x2, local copies, waits for them, and re-layouts  3 us

profile of v6, /device:TPU:1, one launch (start us, length us, event | category | flops | bytes accessed | tf_op | source)
XLA Modules:
  0.0 68.2 jit_solution(7648472527628742550)
XLA Ops:
  0.6 64.6 %shard_map.59 = (f32[3,5,3,16,128]{4,3,2,1,0:T(8,128)}, f32[3,128]{1,0:T(4,128)}) custom-call(bf16[3,20,128,128]{3,2,1,0:T(8,128)(2,1)} %bitcast.2, s32[3,20]{1,0:T(4,128)} %tip_lists.1, s32[3]{0:T(128)} %counts.1, bf16[1,4096]{1,0:T(2,128)(2,1)} %resid_hbm.1), custom_call_target="tpu_custom_call" | custom-call | tf_op jit(solution)/shard_map/pallas_call | solution.py:537
  65.2 1.8 %copy.8 = f32[3,5,3,16,128]{4,3,2,1,0:T(8,128)} copy(f32[3,5,3,16,128]{4,3,2,1,0:T(8,128)} %get-tuple-element.8) | data formatting | bytes 737280
  67.0 1.2 %copy.9 = f32[384]{0:T(512)} copy(f32[384]{0:T(512)} %bitcast.3) | data formatting | bytes 3072

commit v7 on v6

--- a/solution.py
+++ b/solution.py
@@ -110,7 +110,13 @@
         def step(i, carry):
             even, odd = raw[b][tab_smem[1, b, i]], raw[b][tab_smem[1, 4 + b, i]]
             pk0[b][i], pk1[b][i] = even, odd
-            turned0[b][i], turned1[b][i] = even.T, odd.T
+            return carry
+
+        lax.fori_loop(0, half, step, 0, unroll=2)
+
+    def pack_turned(b):
+        def step(i, carry):
+            turned0[b][i], turned1[b][i] = pk0[b][i].T, pk1[b][i].T
             return carry
 
         lax.fori_loop(0, half, step, 0, unroll=2)
@@ -147,7 +153,6 @@
         if b > 0:
             pack(b)
         d_copy[b].start()
-        u_copy[b].start()
 
         @pl.when(hi == 1)
         def _():
@@ -157,6 +162,8 @@
         def _():
             a_copy1[b].start()
 
+        pack_turned(b)
+        u_copy[b].start()
         if b == 0:
             for cp in t_copy:
                 cp.start()
@@ -295,7 +302,8 @@
                     new.append(jnp.where(line == i, power, known))
                 return tuple(new)
 
-            powers = lax.fori_loop(0, n, code, (jnp.zeros((SCALE_ROWS, 128), jnp.float32),) * (NY - 1))
+            powers = lax.fori_loop(0, n, code, (jnp.zeros((SCALE_ROWS, 128), jnp.float32),) * (NY - 1),
+                                   unroll=2 if n % 2 == 0 else 3)
             for part, power in zip(parts, powers):
                 dst = pl.multiple_of(coded_base(u) + part * y_part(u) + n * 32, 16)
                 coded[pl.ds(dst, SCALE_ROWS)] = power.astype(jnp.int32).astype(jnp.int16)
@@ -324,7 +332,7 @@
                 y_sum[pl.ds(pl.multiple_of(BASE[u] * 32 + i * 32, 32), 32)] = total
                 return carry
 
-            lax.fori_loop(0, n, step, 0)
+            lax.fori_loop(0, n, step, 0, unroll=2 if n % 2 == 0 else 3)
             each(u, False, lambda cp: cp.start())
 
         on(u, body)

time: 68.5 us -> 68.4 us (level)
  no operation moved by 1% of the time
where the time goes in v7:
time: 68.4 us; the launch traced here: 68.1 us
  Pallas kernels  64.5 us (94%)
  local copies, waits for them, and re-layouts  3 us (4%)
    pallas_call x1, Pallas kernels, on_device(): pl.pallas_call(band_kernel, out_shape=(jax.ShapeDtypeStruct((blocks, SHIF...  64.5 us
    unnamed x2, local copies, waits for them, and re-layouts  3 us

profile of v7, /device:TPU:1, one launch (start us, length us, event | category | flops | bytes accessed | tf_op | source)
XLA Modules:
  0.0 68.1 jit_solution(428964791781623183)
XLA Ops:
  0.6 64.5 %shard_map.59 = (f32[3,5,3,16,128]{4,3,2,1,0:T(8,128)}, f32[3,128]{1,0:T(4,128)}) custom-call(bf16[3,20,128,128]{3,2,1,0:T(8,128)(2,1)} %bitcast.2, s32[3,20]{1,0:T(4,128)} %tip_lists.1, s32[3]{0:T(128)} %counts.1, bf16[1,4096]{1,0:T(2,128)(2,1)} %resid_hbm.1), custom_call_target="tpu_custom_call" | custom-call | tf_op jit(solution)/shard_map/pallas_call | solution.py:545
  65.1 1.8 %copy.8 = f32[3,5,3,16,128]{4,3,2,1,0:T(8,128)} copy(f32[3,5,3,16,128]{4,3,2,1,0:T(8,128)} %get-tuple-element.8) | data formatting | bytes 737280
  66.9 1.2 %copy.9 = f32[384]{0:T(512)} copy(f32[384]{0:T(512)} %bitcast.3) | data formatting | bytes 3072
